TPU v7x, 128 devices: a whole 4x4x4 slice. The times are simulated.
128 devices in a mesh: sx: 8 (over z, core), sy: 8 (over x_lo, y), rep: 2 (over x_hi).
Axes of the slice: x: 4 (x_hi: 2, x_lo: 2; x = x_hi * 2 + x_lo), y: 4, z: 4, core: 2. Of those that a mesh axis runs over, the one named last changes fastest.
Arguments:
- volume: bfloat16 [2, 32, 16, 128, 256], P('rep', None, 'sx', 'sy'), may hold values from -6 to 6
- first_kernel: bfloat16 [64, 32, 3, 3, 3], replicated, may hold values from -0.21875 to 0.21875
- first_bias: float32 [64], replicated, may hold values from -3 to 3
- second_kernel: bfloat16 [128, 64, 3, 3, 3], P('sy'), may hold values from -0.15625 to 0.15625
- second_bias: float32 [128], P('sy'), may hold values from -3 to 3
- cotangent: bfloat16 [2, 128, 8, 64, 128], P('rep', 'sy', 'sx'), may hold values from -6 to 6
Outputs:
- second_out: float32 [2, 128, 8, 64, 128], P('rep', 'sy', 'sx')
- grad_first_kernel: float32 [64, 32, 3, 3, 3], replicated
- grad_first_bias: float32 [64], replicated
- grad_second_kernel: float32 [128, 64, 3, 3, 3], P('sy')
- grad_second_bias: float32 [128], P('sy')
All inputs are finite; a program needn't handle non-finite values.
Results may differ from a plain program's by a relative error of at most 0.0045.
Values may be sent and summed in bfloat16 or wider, within the bound.
A program may use at most 128 MiB of HBM per device.

v0:
```python
import math

import jax
import jax.numpy as jnp
from jax import lax
from jax.sharding import PartitionSpec as P


def padded_2(cells, sides, width):
    for axis, dim in sides:
        count = lax.axis_size(axis)
        ends = count - 1
        head = lax.slice_in_dim(cells, 0, width, axis=dim)
        tail = lax.slice_in_dim(cells, cells.shape[dim] - width, cells.shape[dim], axis=dim)
        cells = jnp.concatenate(
            [
                lax.ppermute(tail, axis, [(i, (i + 1) % count) for i in range(ends)]),
                cells,
                lax.ppermute(head, axis, [((i + 1) % count, i) for i in range(ends)]),
            ],
            axis=dim,
        )
    return cells


def convolve(padded, kernel, z_pad):
    return lax.conv_general_dilated(
        padded[None],
        kernel,
        (1, 1, 1),
        ((0, 0), (0, 0), (z_pad, z_pad)),
        dimension_numbers=("NCDHW", "OIDHW", "NCDHW"),
        preferred_element_type=jnp.float32,
    )[0]


def weight_terms(cotan, padded):
    cells_x, cells_y, cells_z = (cotan.shape[1], cotan.shape[2], cotan.shape[3])
    terms = []
    for i in range(3):
        for j in range(3):
            for k in range(3):
                piece = padded[:, i : i + cells_x, j : j + cells_y, k : k + cells_z]
                terms.append(
                    jnp.einsum("oxyz,cxyz->oc", cotan, piece, preferred_element_type=jnp.float32)
                )
    stacked = jnp.stack(terms).reshape(3, 3, 3, cotan.shape[0], padded.shape[0])
    return stacked.transpose(3, 4, 0, 1, 2)


def pool_mean(field):
    chans, cells_x, cells_y, cells_z = field.shape
    blocks = field.astype(jnp.float32).reshape(
        chans, cells_x // 2, 2, cells_y // 2, 2, cells_z // 2, 2
    )
    return jnp.mean(blocks, axis=(2, 4, 6))


def per_device(volume, first_kernel, first_bias, second_kernel, second_bias, cotangent):
    source = volume[0]
    cotan = cotangent[0]
    half_x, half_y, half_z = (source.shape[1] // 2, source.shape[2] // 2, source.shape[3] // 2)
    count = (
        lax.axis_size("rep") * lax.axis_size("sx") * lax.axis_size("sy") * half_x * half_y * half_z
    )
    scale = 1.0 / math.sqrt(count)
    rimmed = padded_2(source, (("sx", 1), ("sy", 2)), 1)
    input_pad = jnp.pad(rimmed, ((0, 0), (0, 0), (0, 0), (1, 1)))
    pre = convolve(input_pad, first_kernel, 0) + first_bias[:, None, None, None]
    act = jnp.where(pre > 0, pre, 0.3 * pre)
    pooled = pool_mean(act).astype(jnp.bfloat16)
    pooled_x = padded_2(pooled, (("sx", 1),), 1)
    gathered = lax.all_gather(pooled_x, "sy", axis=2, tiled=True)
    pooled_pad = jnp.pad(gathered, ((0, 0), (0, 0), (1, 1), (1, 1)))
    second = convolve(pooled_pad, second_kernel, 0) + second_bias[:, None, None, None]
    second_out = second.astype(jnp.float32)
    local_w2 = weight_terms(cotan, pooled_pad)
    local_b2 = jnp.sum(cotan.astype(jnp.float32), axis=(1, 2, 3))
    cot_x = padded_2(cotan, (("sx", 1),), 1)
    cot_pad = jnp.pad(cot_x, ((0, 0), (0, 0), (1, 1), (1, 1)))
    flipped = second_kernel.transpose(1, 0, 2, 3, 4)[:, :, ::-1, ::-1, ::-1]
    partial_back = convolve(cot_pad, flipped, 0)
    back = lax.psum_scatter(partial_back, "sy", scatter_dimension=2, tiled=True)
    summed_w2, summed_b2 = lax.psum((local_w2, local_b2), ("sx", "rep"))
    spread = jnp.repeat(jnp.repeat(jnp.repeat(back, 2, axis=1), 2, axis=2), 2, axis=3)
    grad_pre = (spread * 0.125 * jnp.where(pre > 0, 1.0, 0.3)).astype(jnp.bfloat16)
    local_w1 = weight_terms(grad_pre, input_pad)
    local_b1 = jnp.sum(grad_pre.astype(jnp.float32), axis=(1, 2, 3))
    summed_w1, summed_b1 = lax.psum((local_w1, local_b1), ("sx", "sy", "rep"))
    return (
        second_out[None],
        scale * summed_w1,
        scale * summed_b1,
        scale * summed_w2,
        scale * summed_b2,
    )


def solution(mesh):
    placed = (
        P("rep", None, "sx", "sy", None),
        P(),
        P(),
        P("sy", None, None, None, None),
        P("sy"),
        P("rep", "sy", "sx", None, None),
    )
    return jax.shard_map(
        per_device,
        mesh=mesh,
        in_specs=placed,
        out_specs=(
            P("rep", "sy", "sx", None, None),
            P(),
            P(),
            P("sy", None, None, None, None),
            P("sy"),
        ),
        check_vma=False,
    )
```

profile of v0, /device:TPU:1, one launch (start us, length us, event | category | flops | bytes accessed | tf_op | source)
XLA Modules:
  0.0 535.4 jit_solution(5171773666828313169)
XLA Ops:
  8.7 4.9 collective-permute-start.6
  15.5 4.2 collective-permute-done.6
  19.7 4.4 collective-permute-done.7
  25.9 6.1 %copy.331 = bf16[16,3,66,1,8,17]{0,4,5,2,1,3:T(8,128)(2,1)} copy(bf16[16,3,66,1,8,17]{2,0,5,4,1,3:T(8,128)(2,1)S(1)} %bitcast.640) | data formatting | bytes 1723392 | tf_op jit(solution)/shard_map/conv_general_dilated | solution.py:27
  33.4 9.5 %broadcast_select_fusion = f32[1,64,8,17,64]{4,2,3,1,0:T(8,128)S(1)} fusion(pred[8,17]{0,1:T(8,128)(4,1)S(1)} %copy-done.20, bf16[16,64,3,3,3]{1,0,4,3,2:T(8,128)(2,1)S(1)} %copy-done.17, bf16[16,3,66,1,7,2]{0,4,5,2,1,3:T(8,128)(2,1)S(1)} %slice.266, bf16[16,3,66,1,8,17]{0,4,5,2,1,3:T(8,128)(2,1)} %copy.331), kind=kOutput, calls=%fused_computation.70 | convolution fusion | flops 484742656 | bytes 3234056 | tf_op jit(solution)/shard_map/conv_general_dilated | solution.py:27
  52.9 4.7 collective-permute-done.1
  63.5 4.2 collective-permute-done.3
  69.6 5.4 %reshape.246 = bf16[32,4,18,1,8,33]{5,4,0,2,1,3:T(8,128)(2,1)} reshape(bf16[32,4,18,1,264]{4,0,2,1,3:T(8,128)(2,1)S(1)} %pad.15) | data formatting | bytes 2433024 | tf_op jit(solution)/shard_map/conv_general_dilated | solution.py:27
  75.0 9.3 %copy.321 = bf16[32,4,18,1,8,33]{0,4,5,2,1,3:T(8,128)(2,1)} copy(bf16[32,4,18,1,8,33]{5,4,0,2,1,3:T(8,128)(2,1)} %reshape.246) | data formatting | bytes 2433024 | tf_op jit(solution)/shard_map/conv_general_dilated | solution.py:27
  85.4 12.4 %compare_select_fusion = (f32[2,16,8,33,64]{4,2,3,1,0:T(8,128)}, f32[2,16,8,33,64]{4,2,3,1,0:T(8,128)S(1)}, f32[2,16,8,33,64]{4,2,3,1,0:T(8,128)}) fusion(f32[64]{0:T(128)S(1)} %copy-done.15, bf16[64,32,3,3,3]{0,1,4,3,2:T(8,128)(2,1)S(1)} %copy-done, bf16[32,4,18,1,7,2]{0,4,5,2,1,3:T(8,128)(2,1)S(1)} %slice.262, bf16[32,4,18,1,8,33]{0,4,5,2,1,3:T(8,128)(2,1)} %copy.321, ...), kind=kOutput, calls=%fused_computation.44 | convolution fusion | flops 941395968 | bytes 7880200 | tf_op jit(solution)/shard_map/conv_general_dilated | solution.py:27
  104.2 3.3 collective-permute-start.4
  114.9 5.1 copy.419
  120.0 5.1 copy.349
  126.7 11.1 %select_maximum_fusion = bf16[32,4,18,258]{3,0,2,1:T(8,128)(2,1)} fusion(bf16[32,4,1,256]{3,0,2,1:T(8,128)(2,1)S(1)} %collective-permute-done.3, bf16[32,4,1,256]{3,0,2,1:T(8,128)(2,1)S(1)} %collective-permute-done.2, bf16[32,1,16,256]{3,0,2,1:T(8,128)(2,1)S(1)} %collective-permute-done.1, bf16[32,2,16,256]{3,0,2,1:T(8,128)(2,1)S(1)} %bitcast.630, ...), kind=kLoop, calls=%fused_computation.77 | loop fusion | flops 10699776 | bytes 2368512 | tf_op jit(solution)/shard_map/concatenate | solution.py:15
  182.9 36.2 %psum.31 = f32[16]{0:T(128)S(1)} all-reduce(f32[16]{0:T(128)S(1)} %convert_reduce_fusion.1), channel_id=1, replica_groups=mesh['sx'=8,'sy'=8,'rep'=2] {'sx','rep'}, use_global_device_ids=true, to_apply=%region_8.9 | all-reduce | flops 16 | bytes 128 | tf_op jit(solution)/shard_map/psum | solution.py:84
  219.7 66.4 %psum.29 = f32[64]{0:T(128)S(1)} all-reduce(f32[64]{0:T(128)S(1)} %get-tuple-element.30), channel_id=1, replica_groups=mesh['sx'=8,'sy'=8,'rep'=2] {'sx','sy','rep'}, use_global_device_ids=true, to_apply=%region_5.6 | all-reduce | flops 64 | bytes 512 | tf_op jit(solution)/shard_map/psum | solution.py:89
  286.6 41.3 %all-reduce.6.cloned.1.call-done = f32[64,32,3,3,3]{0,1,4,3,2:T(8,128)} async-done(((f32[64,32,3,3,3]{0,1,4,3,2:T(8,128)}), f32[64,32,3,3,3]{0,1,4,3,2:T(8,128)}) %all-reduce.6.cloned.1.call-update) | async-done | bytes 221200 | tf_op jit(solution)/shard_map/psum | solution.py:89
  329.7 40.3 %all-gather.2.cloned.1.call-done = bf16[64,3,64,128]{3,0,2,1:T(8,128)(2,1)} async-done(((bf16[64,3,8,128]{3,0,2,1:T(8,128)(2,1)}), bf16[64,3,64,128]{3,0,2,1:T(8,128)(2,1)}) %all-gather.2.cloned.1.call-update) | async-done | bytes 3145744 | tf_op jit(solution)/shard_map/all_gather | solution.py:73
  385.5 5.5 %pad_bitcast_fusion = bf16[64,3,66,1,130]{4,0,2,1,3:T(8,128)(2,1)} fusion(bf16[64,3,64,128]{3,0,2,1:T(8,128)(2,1)S(1)} %copy-done.2), kind=kLoop, calls=%fused_computation.24 | loop fusion | bytes 6440448 | tf_op jit(solution)/shard_map/broadcast_in_dim | solution.py:28
  391.0 14.8 %copy.420 = bf16[64,3,66,1,130]{2,0,4,1,3:T(8,128)(2,1)} copy(bf16[64,3,66,1,130]{4,0,2,1,3:T(8,128)(2,1)} %pad_bitcast_fusion) | data formatting | bytes 6589440
  405.8 7.5 %pad.17.clone = bf16[64,3,66,1,136]{2,0,4,1,3:T(8,128)(2,1)} pad(bf16[64,3,66,1,130]{2,0,4,1,3:T(8,128)(2,1)} %copy.420, bf16[]{:T(256)} %constant.6.clone.1), padding=0_0x0_0x0_0x0_0x0_6 | pad | bytes 6741506 | tf_op jit(solution)/shard_map/broadcast_in_dim | solution.py:28
  413.3 11.8 %copy.326 = bf16[64,3,66,1,8,17]{0,4,5,2,1,3:T(8,128)(2,1)} copy(bf16[64,3,66,1,8,17]{2,0,5,4,1,3:T(8,128)(2,1)} %bitcast.623) | data formatting | bytes 6893568 | tf_op jit(solution)/shard_map/conv_general_dilated | solution.py:27
  426.5 19.6 %fusion.9 = f32[1,64,8,17,16]{4,2,3,1,0:T(8,128)} fusion(bf16[16,64,3,3,3]{1,0,4,3,2:T(8,128)(2,1)S(1)} %copy-done.18, bf16[64,3,66,1,7,2]{0,4,5,2,1,3:T(8,128)(2,1)S(1)} %slice.264, bf16[64,3,66,1,8,17]{0,4,5,2,1,3:T(8,128)(2,1)} %copy.326), kind=kOutput, calls=%fused_computation.36 | convolution fusion | flops 492853248 | bytes 4413952 | tf_op jit(solution)/shard_map/conv_general_dilated | solution.py:27
  450.9 75.9 %all-reduce.8.cloned.1.call-done = f32[16,64,3,3,3]{1,0,4,3,2:T(8,128)} async-done(((f32[16,64,3,3,3]{1,0,4,3,2:T(8,128)}), f32[16,64,3,3,3]{1,0,4,3,2:T(8,128)}) %all-reduce.8.cloned.1.call-update) | async-done | bytes 110608 | tf_op jit(solution)/shard_map/psum | solution.py:84
  (157 shorter events, 111.6 us)
Async XLA Ops:
  7.2 78.2 %copy-start = (bf16[64,32,3,3,3]{0,1,4,3,2:T(8,128)(2,1)S(1)}, bf16[64,32,3,3,3]{0,1,4,3,2:T(8,128)(2,1)}, u32[]{:S(2)}) copy-start(bf16[64,32,3,3,3]{0,1,4,3,2:T(8,128)(2,1)} %param.7) | copy-start | bytes 331780
  7.2 130.7 %reduce-scatter.2.cloned.1.call-start = ((), (), s32[]{:S(2)}) async-start(), calls=%async_computation.2 | async-start | bytes 4718592 | tf_op jit(solution)/shard_map/reduce_scatter | solution.py:83
  8.7 11.0 %collective-permute-start.6 = (bf16[16,1,64,128]{2,0,3,1:T(8,128)(2,1)S(1)}, bf16[16,1,64,128]{2,0,3,1:T(8,128)(2,1)S(1)}, u32[]{:S(2)}, u32[]{:S(2)}) collective-permute-start(bf16[16,1,64,128]{2,0,3,1:T(8,128)(2,1)S(1)} %bitcast.641), channel_id=1, source_target_pairs={{0,16},{16,32},{32,48},{48,64},{64,80},{80,96},{96,112},{1,17},{17... | collective-permute-start | bytes 786440 | tf_op jit(solution)/shard_map/ppermute | solution.py:17
  13.6 10.5 %collective-permute-start.7 = (bf16[16,1,64,128]{2,0,3,1:T(8,128)(2,1)S(1)}, bf16[16,1,64,128]{2,0,3,1:T(8,128)(2,1)S(1)}, u32[]{:S(2)}, u32[]{:S(2)}) collective-permute-start(bf16[16,1,64,128]{2,0,3,1:T(8,128)(2,1)S(1)} %bitcast.642), channel_id=1, source_target_pairs={{16,0},{32,16},{48,32},{64,48},{80,64},{96,80},{112,96},{17,1},{33... | collective-permute-start | bytes 786440 | tf_op jit(solution)/shard_map/ppermute | solution.py:19
  25.9 7.5 %copy-start.17 = (bf16[16,64,3,3,3]{1,0,4,3,2:T(8,128)(2,1)S(1)}, bf16[16,64,3,3,3]{1,0,4,3,2:T(8,128)(2,1)}, u32[]{:S(2)}) copy-start(bf16[16,64,3,3,3]{1,0,4,3,2:T(8,128)(2,1)} %param.9) | copy-start | bytes 165892
  25.9 7.5 %copy-start.20 = (pred[8,17]{0,1:T(8,128)(4,1)S(1)}, pred[8,17]{0,1:T(8,128)(4,1)}, u32[]{:S(2)}) copy-start(pred[8,17]{0,1:T(8,128)(4,1)} %constant.43) | copy-start | bytes 412
  46.3 281.6 %all-reduce.6.cloned.1.call-start = ((), (), s32[]{:S(2)}) async-start(), calls=%async_computation.3 | async-start | bytes 884736 | tf_op jit(solution)/shard_map/psum | solution.py:89
  47.7 5.2 collective-permute-start
  49.6 8.0 %collective-permute-start.1 = (bf16[32,1,16,256]{3,0,2,1:T(8,128)(2,1)S(1)}, bf16[32,1,16,256]{3,0,2,1:T(8,128)(2,1)S(1)}, u32[]{:S(2)}, u32[]{:S(2)}) collective-permute-start(bf16[32,1,16,256]{3,0,2,1:T(8,128)(2,1)S(1)} %get-tuple-element.39), channel_id=1, source_target_pairs={{16,0},{32,16},{48,32},{64,48},{80,64},{96,80},{112,96},{17,1},{33... | collective-permute-start | bytes 786440 | tf_op jit(solution)/shard_map/ppermute | solution.py:19
  52.9 14.9 %copy-start.4 = (bf16[32,1,16,256]{3,0,2,1:T(8,128)(2,1)}, bf16[32,1,16,256]{3,0,2,1:T(8,128)(2,1)S(1)}, u32[]{:S(2)}) copy-start(bf16[32,1,16,256]{3,0,2,1:T(8,128)(2,1)S(1)} %collective-permute-done) | copy-start | bytes 786436
  57.6 5.9 %collective-permute-start.2 = (bf16[32,4,1,256]{3,0,2,1:T(8,128)(2,1)S(1)}, bf16[32,4,1,256]{3,0,2,1:T(8,128)(2,1)S(1)}, u32[]{:S(2)}, u32[]{:S(2)}) collective-permute-start(bf16[32,4,1,256]{3,0,2,1:T(8,128)(2,1)S(1)} %get-tuple-element.36), channel_id=1, source_target_pairs={{0,2},{2,4},{4,6},{6,8},{8,10},{10,12},{12,14},{1,3},{3,5},{5,7},{... | collective-permute-start | bytes 196616 | tf_op jit(solution)/shard_map/ppermute | solution.py:17
  60.8 6.9 %collective-permute-start.3 = (bf16[32,4,1,256]{3,0,2,1:T(8,128)(2,1)S(1)}, bf16[32,4,1,256]{3,0,2,1:T(8,128)(2,1)S(1)}, u32[]{:S(2)}, u32[]{:S(2)}) collective-permute-start(bf16[32,4,1,256]{3,0,2,1:T(8,128)(2,1)S(1)} %get-tuple-element.37), channel_id=1, source_target_pairs={{2,0},{4,2},{6,4},{8,6},{10,8},{12,10},{14,12},{3,1},{5,3},{7,5},{... | collective-permute-start | bytes 196616 | tf_op jit(solution)/shard_map/ppermute | solution.py:19
  75.0 10.4 %copy-start.15 = (f32[64]{0:T(128)S(1)}, f32[64]{0:T(128)}, u32[]{:S(2)}) copy-start(f32[64]{0:T(128)} %param.8) | copy-start | bytes 772
  75.0 10.4 %copy-start.19 = (pred[8,33]{0,1:T(8,128)(4,1)S(1)}, pred[8,33]{0,1:T(8,128)(4,1)}, u32[]{:S(2)}) copy-start(pred[8,33]{0,1:T(8,128)(4,1)} %constant.41) | copy-start | bytes 796
  104.2 76.5 %collective-permute-start.4 = (bf16[64,1,8,128]{3,0,2,1:T(8,128)(2,1)}, bf16[64,1,8,128]{3,0,2,1:T(8,128)(2,1)}, u32[]{:S(2)}, u32[]{:S(2)}) collective-permute-start(bf16[64,1,8,128]{3,0,2,1:T(8,128)(2,1)} %fusion.182), channel_id=1, source_target_pairs={{0,16},{16,32},{32,48},{48,64},{64,80},{80,96},{96,112},{1,17},{17... | collective-permute-start | bytes 393224 | tf_op jit(solution)/shard_map/ppermute | solution.py:17
  107.5 73.2 %collective-permute-start.5 = (bf16[64,1,8,128]{3,0,2,1:T(8,128)(2,1)}, bf16[64,1,8,128]{3,0,2,1:T(8,128)(2,1)}, u32[]{:S(2)}, u32[]{:S(2)}) collective-permute-start(bf16[64,1,8,128]{3,0,2,1:T(8,128)(2,1)} %fusion.182), channel_id=1, source_target_pairs={{16,0},{32,16},{48,32},{64,48},{80,64},{96,80},{112,96},{17,1},{33... | collective-permute-start | bytes 393224 | tf_op jit(solution)/shard_map/ppermute | solution.py:19
  120.0 5.1 copy-start.5
  151.9 9.2 %slice-start = ((s8[4325376]{0:T(1024)(128)(4,1)}), s8[4194304]{0:T(1024)(128)(4,1)S(1)}, s32[]{:S(2)}) async-start(s8[4325376]{0:T(1024)(128)(4,1)} %bitcast.635), calls=%async_computation.5 | async-start | bytes 8388608
  156.1 5.1 slice-start.1
  177.3 192.7 %copy-start.3 = (bf16[1,16,1,64,128]{4,3,2,1,0:T(8,128)(2,1)S(1)}, bf16[1,16,1,64,128]{4,3,2,1,0:T(8,128)(2,1)}, u32[]{:S(2)}) copy-start(bf16[1,16,1,64,128]{4,3,2,1,0:T(8,128)(2,1)} %param.11) | copy-start | bytes 786436
  180.7 189.4 %all-gather.2.cloned.1.call-start = ((), (), s32[]{:S(2)}) async-start(), calls=%async_computation.1 | async-start | bytes 3538944 | tf_op jit(solution)/shard_map/all_gather | solution.py:73
  182.6 344.2 %all-reduce.8.cloned.1.call-start = ((), (), s32[]{:S(2)}) async-start(), calls=%async_computation.4 | async-start | bytes 442368 | tf_op jit(solution)/shard_map/psum | solution.py:84
  413.3 13.2 %copy-start.18 = (bf16[16,64,3,3,3]{1,0,4,3,2:T(8,128)(2,1)S(1)}, bf16[16,64,3,3,3]{1,0,4,3,2:T(8,128)(2,1)}, u32[]{:S(2)}) copy-start(bf16[16,64,3,3,3]{1,0,4,3,2:T(8,128)(2,1)} %param.9) | copy-start | bytes 165892
  446.1 82.3 %copy-start.1 = (bf16[64,32,3,3,3]{0,1,4,3,2:T(8,128)(2,1)S(1)}, bf16[64,32,3,3,3]{0,1,4,3,2:T(8,128)(2,1)}, u32[]{:S(2)}) copy-start(bf16[64,32,3,3,3]{0,1,4,3,2:T(8,128)(2,1)} %param.7) | copy-start | bytes 331780
  (11 other events, 26.2 us)
Sparse Core Ops, SparseCore 0:
  46.4 54.4 reduce-scatter.1
  180.8 147.0 all-reduce.5
  330.1 39.8 all-gather.1
  385.7 141.0 all-reduce.7
where the time goes:
time: 545 us; the launch traced here: 535 us
  waiting for transfers between devices  177 us (32%)
  blocking collectives  103 us (19%)
  local copies, waits for them, and re-layouts  97.9 us (18%)
  matrix products  90 us (17%)
  other arithmetic  31.6 us (6%)
  starting transfers between devices  21.1 us (4%)
  between operations  14.8 us (3%)
    psum x1, waiting for transfers between devices, per_device(): summed_w2, summed_b2 = lax.psum((local_w2, local_b2), ('sx', 'rep'))  75.9 us
    psum x1, blocking collectives, per_device(): summed_w1, summed_b1 = lax.psum((local_w1, local_b1), ('sx', 'sy', 'rep'))  66.4 us
    dot_general x54, matrix products, weight_terms(): jnp.einsum('oxyz,cxyz->oc', cotan, piece, preferred_element_type=jnp.floa...  48.6 us
    conv_general_dilated x11, local copies, waits for them, and re-layouts, convolve(): lax.conv_general_dilated(padded[None], kernel, (1, 1, 1), ((0, 0), (0, 0)...  45.9 us
    conv_general_dilated x3, matrix products, convolve(): lax.conv_general_dilated(padded[None], kernel, (1, 1, 1), ((0, 0), (0, 0)...  41.4 us
    psum x1, waiting for transfers between devices, per_device(): summed_w1, summed_b1 = lax.psum((local_w1, local_b1), ('sx', 'sy', 'rep'))  41.3 us
    all_gather x1, waiting for transfers between devices, per_device(): gathered = lax.all_gather(pooled_x, 'sy', axis=2, tiled=True)  40.3 us
    psum x1, blocking collectives, per_device(): summed_w2, summed_b2 = lax.psum((local_w2, local_b2), ('sx', 'rep'))  36.2 us
  transfers between devices with their start and end apart: 12, of which 9 were waited for; matrix products, arithmetic and copies ran while one was open for 33% of the time, Pallas kernels for 0%

commit v1 on v0

v1 whole, which is shorter than its diff:
```python
import math

import jax
import jax.numpy as jnp
from jax import lax
from jax.experimental import pallas as pl
from jax.experimental.pallas import tpu as pltpu
from jax.sharding import PartitionSpec as P

MESH = pl.DeviceIdType.MESH
BF16 = jnp.bfloat16
F32 = jnp.float32
NEIGHBOURS = [(dx, dy) for dx in (-1, 0, 1) for dy in (-1, 0, 1) if (dx, dy) != (0, 0)]
VMEM = pl.BlockSpec(memory_space=pltpu.VMEM)
LIMIT = 60 * 1024 * 1024


def place():
    return lax.axis_index("sx"), lax.axis_index("sy"), lax.axis_index("rep")


def remote(src, dst, send, recv, device):
    return pltpu.make_async_remote_copy(
        src_ref=src, dst_ref=dst, send_sem=send, recv_sem=recv, device_id=device, device_id_type=MESH
    )


def greet(devices):
    barrier = pltpu.get_barrier_semaphore()
    for device in devices:
        pl.semaphore_signal(barrier, inc=1, device_id=device, device_id_type=MESH)
    pl.semaphore_wait(barrier, len(devices))


def halo_copies(src, dst, send, recv):
    sx, sy, rep = place()
    cells_x, cells_y = src.shape[0], src.shape[1]
    rim_x, rim_y = cells_x + 1, cells_y + 1
    copies = []
    for k, (dx, dy) in enumerate(NEIGHBOURS):
        from_x = {1: pl.ds(cells_x - 1, 1), -1: pl.ds(0, 1), 0: pl.ds(0, cells_x)}[dx]
        from_y = {1: pl.ds(cells_y - 1, 1), -1: pl.ds(0, 1), 0: pl.ds(0, cells_y)}[dy]
        to_x = {1: pl.ds(0, 1), -1: pl.ds(rim_x, 1), 0: pl.ds(1, cells_x)}[dx]
        to_y = {1: pl.ds(0, 1), -1: pl.ds(rim_y, 1), 0: pl.ds(1, cells_y)}[dy]
        device = ((sx + (dx + 8)) % 8, (sy + (dy + 8)) % 8, rep)
        copies.append(remote(src.at[from_x, from_y], dst.at[to_x, to_y], send.at[k], recv.at[k], device))
    return copies


def clear_rim(dst):
    sx, sy, _ = place()
    rim_x, rim_y = dst.shape[0] - 1, dst.shape[1] - 1

    @pl.when(sx == 0)
    def _():
        dst[0] = jnp.zeros(dst.shape[1:], dst.dtype)

    @pl.when(sx == 7)
    def _():
        dst[rim_x] = jnp.zeros(dst.shape[1:], dst.dtype)

    @pl.when(sy == 0)
    def _():
        dst[:, 0] = jnp.zeros((dst.shape[0],) + dst.shape[2:], dst.dtype)

    @pl.when(sy == 7)
    def _():
        dst[:, rim_y] = jnp.zeros((dst.shape[0],) + dst.shape[2:], dst.dtype)


def spread_kernel(vol, cot, wf, wb, vol_pad, cot_pad, wf_all, wb_all, local_sem, vs, vr, cs, cr, fs, fr, ws, wr):
    sx, sy, rep = place()
    left, right = (sx + 7) % 8, (sx + 1) % 8
    greet(
        [((sx + (dx + 8)) % 8, (sy + (dy + 8)) % 8, rep) for dx in (-1, 1) for dy in (-1, 0, 1)]
        + [(sx, (sy + d) % 8, rep) for d in range(1, 8)]
    )
    volume_copies = halo_copies(vol, vol_pad, vs, vr)
    for copy in volume_copies:
        copy.start()
    mine = pl.ds(pl.multiple_of(16 * sy, 16), 16)
    exchange = []
    for d in range(1, 8):
        peer = (sy + d) % 8
        copy = remote(
            cot.at[pl.ds(8 * peer, 10)], cot_pad.at[1, :, mine, :], cs.at[d], cr.at[d], (sx, peer, rep)
        )
        copy.start()
        exchange.append(copy)
    own_cot = cot.at[pl.ds(8 * sy, 10)]
    locals_ = [
        pltpu.make_async_copy(vol, vol_pad.at[pl.ds(1, 2), pl.ds(1, 16)], local_sem.at[0]),
        pltpu.make_async_copy(own_cot, cot_pad.at[1, :, mine, :], local_sem.at[1]),
        pltpu.make_async_copy(wf, wf_all.at[:, mine, :], local_sem.at[2]),
        pltpu.make_async_copy(wb, wb_all.at[:, mine, :], local_sem.at[3]),
    ]
    for copy in locals_:
        copy.start()
    weights = []
    for d in range(1, 8):
        peer = (sx, (sy + d) % 8, rep)
        weights.append(remote(wf, wf_all.at[:, mine, :], ws.at[d], wr.at[d], peer))
        weights.append(remote(wb, wb_all.at[:, mine, :], ws.at[8 + d], wr.at[8 + d], peer))
    for copy in weights:
        copy.start()
    forwards = []
    for d in range(8):
        rows = pl.ds(pl.multiple_of(16 * ((sy + (8 - d)) % 8), 16), 16)
        if d:
            exchange[d - 1].wait_recv()
            source = cot_pad.at[1, :, rows, :]
        else:
            source = own_cot
        forwards.append(remote(source, cot_pad.at[2, :, rows, :], fs.at[d], fr.at[d], (left, sy, rep)))
        forwards.append(remote(source, cot_pad.at[0, :, rows, :], fs.at[8 + d], fr.at[8 + d], (right, sy, rep)))
        forwards[-2].start()
        forwards[-1].start()
    for copy in locals_ + volume_copies + weights + forwards:
        copy.wait()
    for copy in exchange:
        copy.wait_send()
    clear_rim(vol_pad)

    @pl.when(sx == 0)
    def _():
        cot_pad[0] = jnp.zeros(cot_pad.shape[1:], BF16)

    @pl.when(sx == 7)
    def _():
        cot_pad[2] = jnp.zeros(cot_pad.shape[1:], BF16)


def halo_kernel(src, dst, local_sem, send, recv):
    sx, sy, rep = place()
    greet([((sx + (dx + 8)) % 8, (sy + (dy + 8)) % 8, rep) for dx, dy in NEIGHBOURS])
    copies = halo_copies(src, dst, send, recv)
    for copy in copies:
        copy.start()
    own = pltpu.make_async_copy(src, dst.at[pl.ds(1, 1), pl.ds(1, 8)], local_sem)
    own.start()
    own.wait()
    for copy in copies:
        copy.wait()
    clear_rim(dst)


def shifted(block, step):
    width = block.shape[-1]
    lanes = lax.broadcasted_iota(jnp.int32, block.shape, block.ndim - 1)
    if step == 1:
        return jnp.where(lanes == width - 1, 0.0, pltpu.roll(block, width - 1, block.ndim - 1))
    return jnp.where(lanes == 0, 0.0, pltpu.roll(block, 1, block.ndim - 1))


def combine(stacked, chans):
    return (
        stacked[chans : 2 * chans] + shifted(stacked[:chans], -1) + shifted(stacked[2 * chans :], 1)
    )


def split(block):
    high = block.astype(BF16)
    return high, (block - high.astype(F32)).astype(BF16)


def pairs_of(shape, across):
    rows = lax.broadcasted_iota(jnp.int32, shape, 0)
    columns = lax.broadcasted_iota(jnp.int32, shape, 1)
    hit = (rows // 2 == columns) if across == 0 else (columns // 2 == rows)
    return jnp.where(hit, 1.0, 0.0).astype(BF16)


def first_kernel_body(vol_pad, w1, b1, pooled, mask):
    gather = pairs_of((256, 128), 0)

    def row(y2, carry):
        total = jnp.zeros((64, 256), F32)
        for x in range(2):
            for j in range(2):
                y = 2 * y2 + j
                cells = vol_pad[pl.ds(x, 3), pl.ds(y, 3)].reshape(288, 256)
                pre = combine(jnp.dot(w1[...], cells, preferred_element_type=F32), 64) + b1[...]
                mask[x, y] = jnp.where(pre > 0, 1.0, 0.0).astype(BF16)
                total = total + jnp.where(pre > 0, pre, 0.3 * pre)
        high, low = split(total)
        summed = jnp.dot(high, gather, preferred_element_type=F32) + jnp.dot(
            low, gather, preferred_element_type=F32
        )
        pooled[0, y2] = (summed * 0.125).astype(BF16)
        return carry

    lax.fori_loop(0, 8, row, 0)


def second_kernel_body(vol_pad, cot_pad, wf, wbt, pool_pad, mask, second, gw2, gw1):
    spread = pairs_of((128, 256), 1)
    gw1[...] = jnp.zeros_like(gw1)
    gw2[...] = jnp.zeros_like(gw2)

    def two_rows(ref, y, chans):
        return jnp.concatenate(
            [ref[:, pl.ds(y + j, 3)].reshape(9 * chans, 128) for j in range(2)], axis=1
        )

    def pair(step, carry):
        y2 = 2 * step
        cot_cells = two_rows(cot_pad, y2, 128)
        stacked = jnp.dot(wbt[...], cot_cells, preferred_element_type=F32)
        for j in range(2):
            back = combine(stacked[:, 128 * j : 128 * (j + 1)], 64) * 0.125
            high, low = split(back)
            wide = jnp.dot(high, spread, preferred_element_type=F32) + jnp.dot(
                low, spread, preferred_element_type=F32
            )
            grads, fields = [], []
            bias = jnp.zeros((64, 256), F32)
            for x in range(2):
                for i in range(2):
                    y = 2 * (y2 + j) + i
                    kept = mask[x, y].astype(F32)
                    grad = jnp.where(kept > 0, wide, 0.3 * wide).astype(BF16)
                    exact = grad.astype(F32)
                    bias = bias + exact
                    grads.append(
                        jnp.concatenate(
                            [shifted(exact, 1).astype(BF16), grad, shifted(exact, -1).astype(BF16)], axis=0
                        )
                    )
                    fields.append(vol_pad[pl.ds(x, 3), pl.ds(y, 3)].reshape(288, 256))
            gw1[:, :288] += lax.dot_general(
                jnp.concatenate(grads, axis=1),
                jnp.concatenate(fields, axis=1),
                (((1,), (1,)), ((), ())),
                preferred_element_type=F32,
            )
            gw1[64:128, 288:289] += jnp.sum(bias, axis=1, keepdims=True)
        pool_cells = two_rows(pool_pad, y2, 64)
        stacked = jnp.dot(wf[...], pool_cells, preferred_element_type=F32)
        own = []
        for j in range(2):
            second[y2 + j] = combine(stacked[:, 128 * j : 128 * (j + 1)], 128)
            cot = cot_pad[1, y2 + j + 1].astype(F32)
            gw2[128:256, 576:577] += jnp.sum(cot, axis=1, keepdims=True)
            own.append(
                jnp.concatenate([shifted(cot, 1), cot, shifted(cot, -1)], axis=0).astype(BF16)
            )
        gw2[:, :576] += lax.dot_general(
            jnp.concatenate(own, axis=1), pool_cells, (((1,), (1,)), ((), ())), preferred_element_type=F32
        )
        return carry

    lax.fori_loop(0, 4, pair, 0)


def reduce_kernel(
    scale, second, gw2, gw1, b2, second_out, w2_out, w1_out,
    send2, send1, recv2, recv1, part, parts, whole, all1, local_sem,
    os_, or_, s2, r2, s1, r1, ts, tr, gs, gr, us, ur,
):
    sx, sy, rep = place()
    group = sx * 2 + rep
    peers = [(sx, (sy + d) % 8, rep) for d in range(1, 8)]
    mates = []
    for e in range(1, 16):
        other = (group + e) % 16
        mates.append((other // 2, sy, other % 2))
    send2[...] = gw2[...].astype(BF16)
    for j in range(8):
        send1[j, 0:24] = gw1[24 * j : 24 * (j + 1)].astype(BF16)
        send1[j, 24:32] = jnp.zeros((8, 384), BF16)
    part[...] = jnp.zeros_like(part)
    greet(peers + mates)
    first = []
    for d in range(1, 8):
        j = (sy + d) % 8
        rows = pl.ds(pl.multiple_of(16 * j, 16), 16)
        first.append(remote(send2.at[:, rows, :], recv2.at[d], s2.at[d], r2.at[d], peers[d - 1]))
        first.append(remote(send1.at[j], recv1.at[d], s1.at[d], r1.at[d], peers[d - 1]))
    for copy in first:
        copy.start()
    here = pl.ds(pl.multiple_of(8 * sy, 8), 8)
    outs = []
    for d in range(1, 8):
        rows = pl.ds(pl.multiple_of(16 * ((sy + d) % 8), 16), 16)
        outs.append(remote(second.at[rows], second_out.at[:, here, :], os_.at[d], or_.at[d], peers[d - 1]))
    for copy in outs:
        copy.start()
    mine = pl.ds(pl.multiple_of(16 * sy, 16), 16)
    kept = pltpu.make_async_copy(second.at[mine], second_out.at[:, here, :], local_sem)
    kept.start()
    for copy in first:
        copy.wait()
    sum2 = gw2[:, mine, :]
    sum1 = gw1[pl.ds(pl.multiple_of(24 * sy, 8), 24), :]
    for d in range(1, 8):
        sum2 = sum2 + recv2[d].astype(F32)
        sum1 = sum1 + recv1[d, 0:24].astype(F32)
    for k in range(3):
        for h in range(2):
            for l in range(5):
                part[(k * 2 + h) * 5 + l] = sum2[k, 8 * h : 8 * h + 8, 128 * l : 128 * (l + 1)]
    for r in range(3):
        for l in range(3):
            part[30 + r * 3 + l] = sum1[8 * r : 8 * r + 8, 128 * l : 128 * (l + 1)]
    second_phase = []
    for e in range(1, 16):
        other = (group + e) % 16
        second_phase.append(
            remote(part.at[pl.ds(3 * other, 3)], parts.at[e], ts.at[e], tr.at[e], mates[e - 1])
        )
    for copy in second_phase:
        copy.start()
    kept.wait()
    for copy in outs:
        copy.wait()
    second_out[...] += b2[...]
    for copy in second_phase:
        copy.wait()
    own = pl.ds(3 * group, 3)
    total = part[own]
    for e in range(1, 16):
        total = total + parts[e]
    whole[own] = total * scale
    third = []
    for e in range(1, 16):
        third.append(remote(whole.at[own], whole.at[own], gs.at[e], gr.at[e], mates[e - 1]))
    for copy in third:
        copy.start()
    for copy in third:
        copy.wait()
    last = []
    for d in range(1, 8):
        last.append(remote(whole.at[pl.ds(30, 9)], all1.at[sy], us.at[d], ur.at[d], peers[d - 1]))
    for copy in last:
        copy.start()
    all1[sy] = whole[30:39]
    for k in range(3):
        for h in range(2):
            for l in range(5):
                w2_out[k, 8 * h : 8 * h + 8, 128 * l : 128 * (l + 1)] = whole[(k * 2 + h) * 5 + l]
    for copy in last:
        copy.wait()
    for j in range(8):
        for r in range(3):
            for l in range(3):
                w1_out[24 * j + 8 * r : 24 * j + 8 * r + 8, 128 * l : 128 * (l + 1)] = all1[j, r * 3 + l]


def call(body, outs, scratch=(), collective=None, count=1):
    params = dict(vmem_limit_bytes=LIMIT)
    if collective is not None:
        params.update(collective_id=collective, has_side_effects=True)
    return pl.pallas_call(
        body,
        out_shape=tuple(jax.ShapeDtypeStruct(s, t) for s, t in outs),
        in_specs=[VMEM] * count,
        out_specs=tuple([VMEM] * len(outs)),
        scratch_shapes=list(scratch),
        compiler_params=pltpu.CompilerParams(**params),
    )


def dma(n):
    return pltpu.SemaphoreType.DMA((n,))


def per_device(volume, first_kernel, first_bias, second_kernel, second_bias, cotangent):
    scale = 1.0 / math.sqrt(131072)
    vol = volume[0].transpose(1, 2, 0, 3)
    cot = jnp.pad(cotangent[0, :, 0].transpose(1, 0, 2), ((1, 1), (0, 0), (0, 0)))
    w1 = first_kernel.transpose(4, 0, 2, 3, 1).reshape(192, 288)
    wf = second_kernel.transpose(4, 0, 2, 3, 1).reshape(3, 16, 576)
    wb = second_kernel[:, :, ::-1, ::-1, ::-1].transpose(2, 3, 0, 4, 1).reshape(9, 16, 192)
    vol_pad, cot_pad, wf_all, wb_all = call(
        spread_kernel,
        [((4, 18, 32, 256), BF16), ((3, 10, 128, 128), BF16), ((3, 128, 576), BF16), ((9, 128, 192), BF16)],
        [dma(4), dma(8), dma(8), dma(8), dma(8), dma(16), dma(16), dma(16), dma(16)],
        0,
        4,
    )(vol, cot, wf, wb)
    pooled, mask = call(
        first_kernel_body, [((1, 8, 64, 128), BF16), ((2, 16, 64, 256), BF16)], count=3
    )(vol_pad, w1, first_bias[:, None])
    (pool_pad,) = call(
        halo_kernel, [((3, 10, 64, 128), BF16)], [pltpu.SemaphoreType.DMA, dma(8), dma(8)], 1
    )(pooled)
    wbt = wb_all.reshape(1152, 192).T
    second, gw2, gw1 = call(
        second_kernel_body, [((8, 128, 128), F32), ((384, 640), F32), ((192, 384), F32)], count=6
    )(vol_pad, cot_pad, wf_all.reshape(384, 576), wbt, pool_pad, mask)
    second_out, w2_sum, w1_sum = call(
        lambda *refs: reduce_kernel(scale, *refs),
        [((16, 64, 128), F32), ((3, 16, 640), F32), ((192, 384), F32)],
        [
            pltpu.VMEM((3, 128, 640), BF16),
            pltpu.VMEM((8, 32, 384), BF16),
            pltpu.VMEM((8, 3, 16, 640), BF16),
            pltpu.VMEM((8, 32, 384), BF16),
            pltpu.VMEM((48, 8, 128), F32),
            pltpu.VMEM((16, 3, 8, 128), F32),
            pltpu.VMEM((48, 8, 128), F32),
            pltpu.VMEM((8, 9, 8, 128), F32),
            pltpu.SemaphoreType.DMA,
        ]
        + [dma(8)] * 6
        + [dma(16)] * 4
        + [dma(8)] * 2,
        2,
        4,
    )(second.transpose(1, 0, 2), gw2.reshape(3, 128, 640), gw1, second_bias[:, None, None])
    gw2_out = w2_sum[:, :, :576].reshape(3, 16, 3, 3, 64).transpose(1, 4, 2, 3, 0)
    gw1_out = w1_sum[:, :288].reshape(3, 64, 3, 3, 32).transpose(1, 4, 2, 3, 0)
    return (
        second_out[None, :, None],
        gw1_out,
        w1_sum[64:128, 288],
        gw2_out,
        w2_sum[1, :, 576],
    )


def solution(mesh):
    placed = (
        P("rep", None, "sx", "sy", None),
        P(),
        P(),
        P("sy", None, None, None, None),
        P("sy"),
        P("rep", "sy", "sx", None, None),
    )
    return jax.shard_map(
        per_device,
        mesh=mesh,
        in_specs=placed,
        out_specs=(
            P("rep", "sy", "sx", None, None),
            P(),
            P(),
            P("sy", None, None, None, None),
            P("sy"),
        ),
        check_vma=False,
    )
```

time: 545 us -> 114 us (0.21); the launches traced: 535 us -> 113 us
  waiting for transfers between devices: 177 us -> 0 us
  blocking collectives: 103 us -> 0 us
  Pallas kernels: 0 us -> 96.2 us
  matrix products: 90 us -> 0 us
  local copies, waits for them, and re-layouts: 97.9 us -> 16.3 us
  other arithmetic: 31.6 us -> 0 us
  starting transfers between devices: 21.1 us -> 0 us
  between operations: 14.8 us -> 0.77 us
    psum x2 -> x0, waiting for transfers between devices: 117 us -> none  [the longest x1 75.9 us: per_device(): summed_w2, summed_b2 = lax.psum((local_w2, local_b2), ('sx', 'rep'))]
    psum x2 -> x0, blocking collectives: 103 us -> none  [the longest x1 66.4 us: per_device(): summed_w1, summed_b1 = lax.psum((local_w1, local_b1), ('sx', 'sy', 'rep'))]
    pallas_call x0 -> x5, Pallas kernels: none -> 96.2 us  [the longest x1 39.2 us: per_device(): call(lambda *refs: reduce_kernel(scale, *refs), [((16, 64, 128), F32), ((...]
    dot_general x54 -> x0, matrix products: 48.6 us -> none  [weight_terms(): jnp.einsum('oxyz,cxyz->oc', cotan, piece, preferred_element_type=jnp.floa...]
    conv_general_dilated x11 -> x0, local copies, waits for them, and re-layouts: 45.9 us -> none  [convolve(): lax.conv_general_dilated(padded[None], kernel, (1, 1, 1), ((0, 0), (0, 0)...]
    conv_general_dilated x3 -> x0, matrix products: 41.4 us -> none  [convolve(): lax.conv_general_dilated(padded[None], kernel, (1, 1, 1), ((0, 0), (0, 0)...]
    all_gather x1 -> x0, waiting for transfers between devices: 40.3 us -> none  [per_device(): gathered = lax.all_gather(pooled_x, 'sy', axis=2, tiled=True)]
    unnamed x51 -> x21, local copies, waits for them, and re-layouts: 25.9 us -> 4.61 us
  transfers between devices with their start and end apart: 12 -> 0, of which waited for: 9 -> 0; matrix products, arithmetic and copies ran while one was open for 33% -> 0% of each run, Pallas kernels for 0% -> 0%
where the time goes in v1:
time: 114 us; the launch traced here: 113 us
  Pallas kernels  96.2 us (84%)
  local copies, waits for them, and re-layouts  16.3 us (14%)
    pallas_call x1, Pallas kernels, per_device(): call(lambda *refs: reduce_kernel(scale, *refs), [((16, 64, 128), F32), ((...  39.2 us
    pallas_call x1, Pallas kernels, per_device(): call(spread_kernel, [((4, 18, 32, 256), BF16), ((3, 10, 128, 128), BF16),...  27.1 us
    pallas_call x1, Pallas kernels, per_device(): call(halo_kernel, [((3, 10, 64, 128), BF16)], [pltpu.SemaphoreType.DMA, d...  11.6 us
    pallas_call x1, Pallas kernels, per_device(): call(second_kernel_body, [((8, 128, 128), F32), ((384, 640), F32), ((192,...  11.4 us
    pallas_call x1, Pallas kernels, per_device(): call(first_kernel_body, [((1, 8, 64, 128), BF16), ((2, 16, 64, 256), BF16...  6.97 us
    unnamed x21, local copies, waits for them, and re-layouts  4.61 us

profile of v1, /device:TPU:1, one launch (start us, length us, event | category | flops | bytes accessed | tf_op | source)
XLA Modules:
  0.0 113.2 jit_solution(17114853449421295468)
XLA Ops:
  0.7 1.2 %copy.42 = bf16[1,16,1,64,128]{4,1,3,2,0:T(8,128)(2,1)S(1)} copy(bf16[1,16,1,64,128]{4,3,2,1,0:T(8,128)(2,1)} %param.11) | data formatting | bytes 524288 | tf_op args[5]
  1.8 0.7 pad.4.cot
  2.6 1.1 copy.41
  3.7 0.8 reshape.35.wb
  4.6 0.8 reshape.34.wf
  5.4 27.1 %shard_map.101 = (bf16[4,18,32,256]{3,2,1,0:T(8,128)(2,1)}, bf16[3,10,128,128]{3,2,1,0:T(8,128)(2,1)}, bf16[3,128,576]{2,1,0:T(8,128)(2,1)}, bf16[9,128,192]{2,1,0:T(8,128)(2,1)}) custom-call(bf16[2,16,32,256]{3,2,1,0:T(8,128)(2,1)} %bitcast.36, bf16[66,16,128]{2,1,0:T(8,128)(2,1)} %pad.4.cot, bf16[3,16,576]{2,1,0:T(8,128)(2,1)} %reshape.34.wf, ...), custom_call_target="tpu_custom_call" | custom-call | tf_op jit(solution)/shard_map/pallas_call | solution.py:374
  32.4 0.2 copy.28
  32.6 0.2 reshape.38
  32.8 0.8 copy.29.w1
  33.6 0.7 copy.30.b1
  34.3 7.0 %shard_map.102 = (bf16[1,8,64,128]{3,2,1,0:T(8,128)(2,1)}, bf16[2,16,64,256]{3,2,1,0:T(8,128)(2,1)}) custom-call(bf16[4,18,32,256]{3,2,1,0:T(8,128)(2,1)} %get-tuple-element.17.vol_pad, bf16[192,288]{1,0:T(8,128)(2,1)} %copy.29.w1, f32[64,1]{1,0:T(8,128)} %copy.30.b1), custom_call_target="tpu_custom_call" | custom-call | tf_op jit(solution)/shard_map/pallas_call | solution.py:381
  41.3 11.6 %shard_map.103.pool_pad = bf16[3,10,64,128]{3,2,1,0:T(8,128)(2,1)} custom-call(bf16[1,8,64,128]{3,2,1,0:T(8,128)(2,1)} %get-tuple-element.21.src), custom_call_target="tpu_custom_call" | custom-call | tf_op jit(solution)/shard_map/pallas_call | solution.py:384
  52.8 1.0 copy.27
  53.8 11.4 %shard_map.104 = (f32[8,128,128]{2,1,0:T(8,128)}, f32[384,640]{1,0:T(8,128)}, f32[192,384]{1,0:T(8,128)}) custom-call(bf16[4,18,32,256]{3,2,1,0:T(8,128)(2,1)} %get-tuple-element.17.vol_pad, bf16[3,10,128,128]{3,2,1,0:T(8,128)(2,1)} %get-tuple-element.18.cot_pad, bf16[384,576]{1,0:T(8,128)(2,1)} %bitcast.43, bf16[192,1152]{1,0:T(8,128)(2,1)} %bitcast.37, ...), custom_call_target="tpu_custom_call" | custom-call | tf_op jit(solution)/shard_map/pallas_call | solution.py:388
  65.2 2.1 %copy.40 = f32[8,128,128]{2,0,1:T(8,128)} copy(f32[8,128,128]{2,1,0:T(8,128)} %get-tuple-element.23) | data formatting | bytes 1048576 | tf_op jit(solution)/shard_map/pallas_call | solution.py:388
  67.4 0.7 copy.32.refs_3_
  68.1 39.2 %shard_map.105 = (f32[16,64,128]{2,1,0:T(8,128)}, f32[3,16,640]{2,1,0:T(8,128)}, f32[192,384]{1,0:T(8,128)}) custom-call(f32[128,8,128]{2,1,0:T(8,128)} %bitcast.35, f32[3,128,640]{2,1,0:T(8,128)} %bitcast.40, f32[192,384]{1,0:T(8,128)} %get-tuple-element.25.refs_2_, f32[16,1,1]{2,1,0:T(1,128)} %copy.32.refs_3_), custom_call_target="tpu_custom_call" | custom-call | tf_op jit(solution)/shard_map/pallas_call | solution.py:391
  107.3 1.1 %copy.33 = f32[192,288]{0,1:T(8,128)S(1)} copy(f32[192,288]{1,0:T(8,128)} %bitcast.45) | data formatting | bytes 442368 | tf_op jit(solution)/shard_map/slice | solution.py:412
  108.4 0.2 reshape.40
  108.6 0.8 copy.35
  109.6 0.7 copy.36
  110.3 1.5 %slice_reduce_fusion = f32[64]{0:T(128)} fusion(f32[192,384]{1,0:T(8,128)} %get-tuple-element.27), kind=kLoop, calls=%fused_computation.4 | loop fusion | bytes 512 | tf_op jit(solution)/shard_map/slice | solution.py:416
  111.8 0.7 slice_reduce_fusion.1
  112.5 0.8 copy.44
  (20 shorter events, 0.3 us)
Async XLA Ops:
  0.6 1.9 %copy-start.1 = (bf16[1,32,2,16,256]{4,3,2,1,0:T(8,128)(2,1)S(1)}, bf16[1,32,2,16,256]{4,3,2,1,0:T(8,128)(2,1)}, u32[]{:S(2)}) copy-start(bf16[1,32,2,16,256]{4,3,2,1,0:T(8,128)(2,1)} %param.6) | copy-start | bytes 1572868
  0.6 3.0 %copy-start.3 = (bf16[16,64,3,3,3]{1,0,4,3,2:T(8,128)(2,1)S(1)}, bf16[16,64,3,3,3]{1,0,4,3,2:T(8,128)(2,1)}, u32[]{:S(2)}) copy-start(bf16[16,64,3,3,3]{1,0,4,3,2:T(8,128)(2,1)} %param.9) | copy-start | bytes 165892
  3.7 28.8 %copy-start.4 = (bf16[64,32,3,3,3]{0,1,4,3,2:T(8,128)(2,1)S(1)}, bf16[64,32,3,3,3]{0,1,4,3,2:T(8,128)(2,1)}, u32[]{:S(2)}) copy-start(bf16[64,32,3,3,3]{0,1,4,3,2:T(8,128)(2,1)} %param.7) | copy-start | bytes 331780
  4.6 29.0 %copy-start.6 = (f32[64]{0:T(128)S(1)}, f32[64]{0:T(128)}, u32[]{:S(2)}) copy-start(f32[64]{0:T(128)} %param.8) | copy-start | bytes 772
  32.8 20.0 %copy-start = (bf16[9,128,192]{2,1,0:T(8,128)(2,1)S(1)}, bf16[9,128,192]{2,1,0:T(8,128)(2,1)}, u32[]{:S(2)}) copy-start(bf16[9,128,192]{2,1,0:T(8,128)(2,1)} %get-tuple-element.20) | copy-start | bytes 1327108
  53.8 13.5 %copy-start.7 = (f32[16]{0:T(128)S(1)}, f32[16]{0:T(128)}, u32[]{:S(2)}) copy-start(f32[16]{0:T(128)} %param.10) | copy-start | bytes 196
  107.3 2.2 %copy-start.5 = (f32[3,16,640]{2,1,0:T(8,128)S(1)}, f32[3,16,640]{2,1,0:T(8,128)}, u32[]{:S(2)}) copy-start(f32[3,16,640]{2,1,0:T(8,128)} %get-tuple-element.28) | copy-start | bytes 368644
  108.6 3.8 %copy-start.2 = (f32[16,64,128]{2,1,0:T(8,128)S(1)}, f32[16,64,128]{2,1,0:T(8,128)}, u32[]{:S(2)}) copy-start(f32[16,64,128]{2,1,0:T(8,128)} %get-tuple-element.26) | copy-start | bytes 1572868

commit v2 on v0

v2 whole, which is shorter than its diff:
```python
import math

import jax
import jax.numpy as jnp
from jax import lax
from jax.experimental import pallas as pl
from jax.experimental.pallas import tpu as pltpu
from jax.sharding import PartitionSpec as P

MESH = pl.DeviceIdType.MESH
BF16 = jnp.bfloat16
F32 = jnp.float32
NEIGHBOURS = [(dx, dy) for dx in (-1, 0, 1) for dy in (-1, 0, 1) if (dx, dy) != (0, 0)]
VMEM = pl.BlockSpec(memory_space=pltpu.VMEM)
LIMIT = 60 * 1024 * 1024


def place():
    return lax.axis_index("sx"), lax.axis_index("sy"), lax.axis_index("rep")


def remote(src, dst, send, recv, device):
    return pltpu.make_async_remote_copy(
        src_ref=src, dst_ref=dst, send_sem=send, recv_sem=recv, device_id=device, device_id_type=MESH
    )


def greet(devices):
    barrier = pltpu.get_barrier_semaphore()
    for device in devices:
        pl.semaphore_signal(barrier, inc=1, device_id=device, device_id_type=MESH)
    pl.semaphore_wait(barrier, len(devices))


def halo_copies(src, dst, send, recv):
    sx, sy, rep = place()
    cells_x, cells_y = src.shape[0], src.shape[1]
    rim_x, rim_y = cells_x + 1, cells_y + 1
    copies = []
    for k, (dx, dy) in enumerate(NEIGHBOURS):
        from_x = {1: pl.ds(cells_x - 1, 1), -1: pl.ds(0, 1), 0: pl.ds(0, cells_x)}[dx]
        from_y = {1: pl.ds(cells_y - 1, 1), -1: pl.ds(0, 1), 0: pl.ds(0, cells_y)}[dy]
        to_x = {1: pl.ds(0, 1), -1: pl.ds(rim_x, 1), 0: pl.ds(1, cells_x)}[dx]
        to_y = {1: pl.ds(0, 1), -1: pl.ds(rim_y, 1), 0: pl.ds(1, cells_y)}[dy]
        device = ((sx + (dx + 8)) % 8, (sy + (dy + 8)) % 8, rep)
        copies.append(remote(src.at[from_x, from_y], dst.at[to_x, to_y], send.at[k], recv.at[k], device))
    return copies


def clear_rim(dst):
    sx, sy, _ = place()
    rim_x, rim_y = dst.shape[0] - 1, dst.shape[1] - 1

    @pl.when(sx == 0)
    def _():
        dst[0] = jnp.zeros(dst.shape[1:], dst.dtype)

    @pl.when(sx == 7)
    def _():
        dst[rim_x] = jnp.zeros(dst.shape[1:], dst.dtype)

    @pl.when(sy == 0)
    def _():
        dst[:, 0] = jnp.zeros((dst.shape[0],) + dst.shape[2:], dst.dtype)

    @pl.when(sy == 7)
    def _():
        dst[:, rim_y] = jnp.zeros((dst.shape[0],) + dst.shape[2:], dst.dtype)


def shifted(block, step):
    width = block.shape[-1]
    lanes = lax.broadcasted_iota(jnp.int32, block.shape, block.ndim - 1)
    if step == 1:
        return jnp.where(lanes == width - 1, 0.0, pltpu.roll(block, width - 1, block.ndim - 1))
    return jnp.where(lanes == 0, 0.0, pltpu.roll(block, 1, block.ndim - 1))


def combine(stacked, chans):
    return (
        stacked[chans : 2 * chans] + shifted(stacked[:chans], -1) + shifted(stacked[2 * chans :], 1)
    )


def split(block):
    high = block.astype(BF16)
    return high, (block - high.astype(F32)).astype(BF16)


def pairs_of(shape, across):
    rows = lax.broadcasted_iota(jnp.int32, shape, 0)
    columns = lax.broadcasted_iota(jnp.int32, shape, 1)
    hit = (rows // 2 == columns) if across == 0 else (columns // 2 == rows)
    return jnp.where(hit, 1.0, 0.0).astype(BF16)


def first_rows(vol_pad, w1, bias, pooled, mask, start, stop):
    gather = pairs_of((256, 128), 0)

    def row(y2, carry):
        total = jnp.zeros((64, 256), F32)
        for x in range(2):
            for j in range(2):
                y = 2 * y2 + j
                cells = vol_pad[pl.ds(x, 3), pl.ds(y, 3)].reshape(288, 256)
                pre = combine(jnp.dot(w1[0:192, 0:288], cells, preferred_element_type=F32), 64) + bias
                mask[x, y] = jnp.where(pre > 0, 1.0, 0.0).astype(BF16)
                total = total + jnp.where(pre > 0, pre, 0.3 * pre)
        high, low = split(total)
        summed = jnp.dot(high, gather, preferred_element_type=F32) + jnp.dot(
            low, gather, preferred_element_type=F32
        )
        pooled[0, y2] = (summed * 0.125).astype(BF16)
        return carry

    lax.fori_loop(start, stop, row, 0)


def two_rows(ref, y, chans):
    return jnp.concatenate(
        [ref[:, pl.ds(y + j, 3)].reshape(9 * chans, 128) for j in range(2)], axis=1
    )


def across(a, b):
    return lax.dot_general(a, b, (((1,), (1,)), ((), ())), preferred_element_type=F32)


def back_rows(vol_pad, cot_pad, wbt, mask, gw1):
    spread = pairs_of((128, 256), 1)
    ones = jnp.ones((16, 1024), BF16)

    def pair(step, carry):
        y2 = 2 * step
        stacked = jnp.dot(wbt[...], two_rows(cot_pad, y2, 128), preferred_element_type=F32)
        for j in range(2):
            back = combine(stacked[:, 128 * j : 128 * (j + 1)], 64) * 0.125
            high, low = split(back)
            wide = jnp.dot(high, spread, preferred_element_type=F32) + jnp.dot(
                low, spread, preferred_element_type=F32
            )
            grads, fields = [], []
            for x in range(2):
                for i in range(2):
                    y = 2 * (y2 + j) + i
                    kept = mask[x, y].astype(F32)
                    grad = jnp.where(kept > 0, wide, 0.3 * wide)
                    grads.append(
                        jnp.concatenate([shifted(grad, 1), grad, shifted(grad, -1)], axis=0).astype(BF16)
                    )
                    fields.append(vol_pad[pl.ds(x, 3), pl.ds(y, 3)].reshape(288, 256))
            cells = jnp.concatenate([jnp.concatenate(fields, axis=1), ones], axis=0)
            gw1[0:304, 0:192] += across(cells, jnp.concatenate(grads, axis=1))
        return carry

    lax.fori_loop(0, 4, pair, 0)


def second_rows(cot_pad, wf_all, pool_pad, second):
    def pair(step, carry):
        y2 = 2 * step
        weights = wf_all[...].reshape(384, 640)[:, 0:576]
        stacked = jnp.dot(weights, two_rows(pool_pad, y2, 64), preferred_element_type=F32)
        for j in range(2):
            second[y2 + j] = combine(stacked[:, 128 * j : 128 * (j + 1)], 128).astype(BF16)
        return carry

    lax.fori_loop(0, 4, pair, 0)


def second_grads(cot_pad, pool_pad, gw2):
    ones = jnp.ones((16, 256), BF16)

    def pair(step, carry):
        y2 = 2 * step
        cells = jnp.concatenate([two_rows(pool_pad, y2, 64), ones], axis=0)
        own = []
        for j in range(2):
            cot = cot_pad[1, y2 + j + 1].astype(F32)
            own.append(
                jnp.concatenate([shifted(cot, 1), cot, shifted(cot, -1)], axis=0).astype(BF16)
            )
        gw2[:, 0:592] += across(jnp.concatenate(own, axis=1), cells)
        return carry

    lax.fori_loop(0, 4, pair, 0)


def whole_kernel(
    vol, cot, k1, b1, k2, rows_out, gw2_out, gb2_out, gw1_out, gb1_out,
    cot_src, wf_own, vol_pad, cot_pad, wf_all, w1t, w1, wbt, pooled, pool_pad, mask, second, gw1, gw2,
    send1, recv1, part1, parts1, whole1, all1, send2, recv2, part2, parts2, whole2,
    ls, vs, vr, cs, cr, fs, fr, ws, wr, xs, xr, ps, pr, os_, or_,
    s1, r1, t1, q1, g1, h1, u1, v1, s2, r2, t2, q2, g2, h2,
):
    sx, sy, rep = place()
    core = sx % 2
    left, right = (sx + 7) % 8, (sx + 1) % 8
    partner = (sx + 1 - 2 * core, sy, rep)
    group = sx * 2 + rep
    peers = [(sx, (sy + d) % 8, rep) for d in range(1, 8)]
    mates = []
    for e in range(1, 16):
        other = (group + e) % 16
        mates.append((other // 2, sy, other % 2))
    mine = pl.ds(pl.multiple_of(16 * sy, 16), 16)

    def theirs(d):
        return pl.ds(pl.multiple_of(16 * ((sy + d) % 8), 16), 16)

    cot_src[0] = jnp.zeros((16, 128), BF16)
    cot_src[65] = jnp.zeros((16, 128), BF16)
    cot_src[1:65] = cot[...]
    for k in range(9):
        for z in range(3):
            wf_own[z, :, 64 * k : 64 * k + 64] = k2[3 * k + z]
    wf_own[:, :, 576:640] = jnp.zeros((3, 16, 64), BF16)
    greet(
        [((sx + (dx + 8)) % 8, (sy + (dy + 8)) % 8, rep) for dx in (-1, 1) for dy in (-1, 1)]
        + peers
        + mates
    )
    halo = halo_copies(vol, vol_pad, vs, vr)
    for copy in halo:
        copy.start()
    exchange = []
    for d in range(1, 8):
        source = cot_src.at[pl.ds(8 * ((sy + d) % 8), 10)]
        exchange.append(remote(source, cot_pad.at[1, :, mine, :], cs.at[d], cr.at[d], peers[d - 1]))
    for copy in exchange:
        copy.start()
    planes = pl.ds(core, 2)
    weights = []
    for d in range(1, 8):
        weights.append(
            remote(wf_own.at[planes], wf_all.at[planes, mine, :], ws.at[d], wr.at[d], peers[d - 1])
        )
    for copy in weights:
        copy.start()
    own_cot = cot_src.at[pl.ds(8 * sy, 10)]
    locals_ = [
        pltpu.make_async_copy(vol, vol_pad.at[pl.ds(1, 2), pl.ds(1, 16)], ls.at[0]),
        pltpu.make_async_copy(own_cot, cot_pad.at[1, :, mine, :], ls.at[1]),
        pltpu.make_async_copy(wf_own, wf_all.at[:, mine, :], ls.at[2]),
    ]
    for copy in locals_:
        copy.start()
    forwards = []

    def forward(d):
        rows = theirs(8 - d)
        source = cot_pad.at[1, :, rows, :] if d else own_cot
        both = [
            remote(source, cot_pad.at[2, :, rows, :], fs.at[d], fr.at[d], (left, sy, rep)),
            remote(source, cot_pad.at[0, :, rows, :], fs.at[8 + d], fr.at[8 + d], (right, sy, rep)),
        ]
        for copy in both:
            copy.start()
        forwards.extend(both)

    forward(0)
    for k in range(9):
        for z in range(3):
            w1t[32 * k : 32 * k + 32, 64 * z : 64 * z + 64] = k1[3 * k + z]
    w1t[288:384, :] = jnp.zeros((96, 256), BF16)
    w1t[0:288, 192:256] = jnp.zeros((288, 64), BF16)
    w1[...] = w1t[...].T
    square = (64, 64)
    diagonal = lax.broadcasted_iota(jnp.int32, square, 0) == lax.broadcasted_iota(jnp.int32, square, 1)
    bias = jnp.sum(jnp.where(diagonal, b1[...], 0.0), axis=1, keepdims=True)
    gw1[...] = jnp.zeros_like(gw1)
    gw2[...] = jnp.zeros_like(gw2)
    part1[...] = jnp.zeros_like(part1)
    part2[...] = jnp.zeros_like(part2)
    for copy in locals_ + halo:
        copy.wait()
    clear_rim(vol_pad)
    first_rows(vol_pad, w1, bias, pooled, mask, 0, 4)
    for d in range(1, 8):
        exchange[d - 1].wait_recv()
        forward(d)
    first_rows(vol_pad, w1, bias, pooled, mask, 4, 8)
    pool_halo = halo_copies(pooled, pool_pad, ps, pr)
    for copy in pool_halo:
        copy.start()
    pool_pad[1, 1:9] = pooled[0]
    share = []
    plane = pl.ds(2 * core, 1)
    for d in range(1, 8):
        weights[d - 1].wait_recv()
        rows = theirs(8 - d)
        share.append(
            remote(wf_all.at[plane, rows, :], wf_all.at[plane, rows, :], xs.at[d], xr.at[d], partner)
        )
        share[-1].start()
    for copy in forwards + share:
        copy.wait()
    for copy in exchange + weights:
        copy.wait_send()

    @pl.when(sx == 0)
    def _():
        cot_pad[0] = jnp.zeros(cot_pad.shape[1:], BF16)

    @pl.when(sx == 7)
    def _():
        cot_pad[2] = jnp.zeros(cot_pad.shape[1:], BF16)

    for z in range(3):
        turned = wf_all[z].T
        for k in range(9):
            wbt[64 * (2 - z) : 64 * (3 - z), 128 * (8 - k) : 128 * (9 - k)] = turned[64 * k : 64 * k + 64]
    back_rows(vol_pad, cot_pad, wbt, mask, gw1)
    for j in range(8):
        send1[j] = gw1[40 * j : 40 * (j + 1)].astype(BF16)
    first1 = []
    for d in range(1, 8):
        first1.append(remote(send1.at[(sy + d) % 8], recv1.at[d], s1.at[d], r1.at[d], peers[d - 1]))
    for copy in first1:
        copy.start()
    for copy in pool_halo:
        copy.wait()
    clear_rim(pool_pad)
    second_rows(cot_pad, wf_all, pool_pad, second)
    here = pl.ds(pl.multiple_of(8 * sy, 8), 8)
    outs = []
    for d in range(1, 8):
        outs.append(remote(second.at[:, theirs(d), :], rows_out.at[here], os_.at[d], or_.at[d], peers[d - 1]))
    for copy in outs:
        copy.start()
    kept = pltpu.make_async_copy(second.at[:, mine, :], rows_out.at[here], ls.at[3])
    kept.start()
    second_grads(cot_pad, pool_pad, gw2)
    send2[...] = gw2[...].reshape(3, 128, 640).astype(BF16)
    first2 = []
    for d in range(1, 8):
        first2.append(remote(send2.at[:, theirs(d), :], recv2.at[d], s2.at[d], r2.at[d], peers[d - 1]))
    for copy in first2:
        copy.start()
    for copy in first1:
        copy.wait()
    sum1 = gw1[pl.ds(pl.multiple_of(40 * sy, 8), 40), :]
    for d in range(1, 8):
        sum1 = sum1 + recv1[d].astype(F32)
    for r in range(5):
        for l in range(2):
            part1[2 * r + l] = sum1[8 * r : 8 * r + 8, 128 * l : 128 * (l + 1)]
    reduce1 = []
    for e in range(1, 16):
        other = (group + e) % 16
        reduce1.append(remote(part1.at[other], parts1.at[e], t1.at[e], q1.at[e], mates[e - 1]))
    for copy in reduce1:
        copy.start()
    for copy in first2:
        copy.wait()
    sum2 = jnp.concatenate(
        [gw2[pl.ds(pl.multiple_of(128 * z + 16 * sy, 16), 16), :][None] for z in range(3)], axis=0
    )
    for d in range(1, 8):
        sum2 = sum2 + recv2[d].astype(F32)
    for z in range(3):
        for h in range(2):
            for l in range(5):
                part2[(z * 2 + h) * 5 + l] = sum2[z, 8 * h : 8 * h + 8, 128 * l : 128 * (l + 1)]
    reduce2 = []
    for e in range(1, 16):
        other = (group + e) % 16
        reduce2.append(remote(part2.at[pl.ds(2 * other, 2)], parts2.at[e], t2.at[e], q2.at[e], mates[e - 1]))
    for copy in reduce2:
        copy.start()
    for copy in reduce1:
        copy.wait()
    total1 = part1[group]
    for e in range(1, 16):
        total1 = total1 + parts1[e]
    whole1[group] = total1
    gather1 = []
    for e in range(1, 16):
        gather1.append(remote(whole1.at[group], whole1.at[group], g1.at[e], h1.at[e], mates[e - 1]))
    for copy in gather1:
        copy.start()
    for copy in reduce2:
        copy.wait()
    own = pl.ds(2 * group, 2)
    total2 = part2[own]
    for e in range(1, 16):
        total2 = total2 + parts2[e]
    whole2[own] = total2
    gather2 = []
    for e in range(1, 16):
        gather2.append(remote(whole2.at[own], whole2.at[own], g2.at[e], h2.at[e], mates[e - 1]))
    for copy in gather2:
        copy.start()
    for copy in gather1:
        copy.wait()
    last1 = []
    for d in range(1, 8):
        last1.append(remote(whole1.at[pl.ds(0, 10)], all1.at[sy], u1.at[d], v1.at[d], peers[d - 1]))
    for copy in last1:
        copy.start()
    all1[sy] = whole1[0:10]
    for copy in gather2:
        copy.wait()
    for z in range(3):
        for h in range(2):
            for l in range(5):
                tile = whole2[(z * 2 + h) * 5 + l]
                gw2_out[2 * l * 3 + z, 8 * h : 8 * h + 8, :] = tile[:, 0:64]
                if l < 4:
                    gw2_out[(2 * l + 1) * 3 + z, 8 * h : 8 * h + 8, :] = tile[:, 64:128]
    column = jnp.concatenate([whole2[14][:, 64:65], whole2[19][:, 64:65]], axis=0)
    square = (16, 16)
    diagonal = lax.broadcasted_iota(jnp.int32, square, 0) == lax.broadcasted_iota(jnp.int32, square, 1)
    gb2_out[...] = jnp.sum(jnp.where(diagonal, column, 0.0), axis=0, keepdims=True)
    kept.wait()
    for copy in outs:
        copy.wait()
    for copy in last1:
        copy.wait()
    for j in range(8):
        for r in range(5):
            at = 40 * j + 8 * r
            if at < 288:
                for z in range(3):
                    tile = all1[j, 2 * r + z // 2]
                    gw1_out[3 * (at // 32) + z, at % 32 : at % 32 + 8, :] = tile[
                        :, 64 * (z % 2) : 64 * (z % 2) + 64
                    ]
    gb1_out[...] = all1[7, 2][0:1, 64:128]


def dma(n):
    return pltpu.SemaphoreType.DMA((n,))


def per_device(volume, first_kernel, first_bias, second_kernel, second_bias, cotangent):
    scale = 1.0 / math.sqrt(131072)
    vol = volume[0].transpose(1, 2, 0, 3)
    cot = cotangent[0, :, 0].transpose(1, 0, 2)
    k1 = first_kernel.transpose(2, 3, 4, 1, 0).reshape(27, 32, 64)
    k2 = second_kernel.transpose(2, 3, 4, 0, 1).reshape(27, 16, 64)
    outs = [
        ((64, 16, 128), BF16), ((27, 16, 64), F32), ((1, 16), F32), ((27, 32, 64), F32), ((1, 64), F32)
    ]
    scratch = [
        ((66, 16, 128), BF16),
        ((3, 16, 640), BF16),
        ((4, 18, 32, 256), BF16),
        ((3, 10, 128, 128), BF16),
        ((3, 128, 640), BF16),
        ((384, 256), BF16),
        ((256, 384), BF16),
        ((192, 1152), BF16),
        ((1, 8, 64, 128), BF16),
        ((3, 10, 64, 128), BF16),
        ((2, 16, 64, 256), BF16),
        ((8, 128, 128), BF16),
        ((320, 256), F32),
        ((384, 640), F32),
        ((8, 40, 256), BF16),
        ((8, 40, 256), BF16),
        ((16, 8, 128), F32),
        ((16, 8, 128), F32),
        ((16, 8, 128), F32),
        ((8, 10, 8, 128), F32),
        ((3, 128, 640), BF16),
        ((8, 3, 16, 640), BF16),
        ((32, 8, 128), F32),
        ((16, 2, 8, 128), F32),
        ((32, 8, 128), F32),
    ]
    sems = [4, 8, 8, 8, 8, 16, 16, 8, 8, 8, 8, 8, 8, 8, 8, 8, 8, 16, 16, 16, 16, 8, 8, 8, 8, 16, 16, 16, 16]
    rows_out, gw2, gb2, gw1, gb1 = pl.pallas_call(
        whole_kernel,
        out_shape=tuple(jax.ShapeDtypeStruct(s, t) for s, t in outs),
        in_specs=[VMEM] * 5,
        out_specs=tuple([VMEM] * 5),
        scratch_shapes=[pltpu.VMEM(s, t) for s, t in scratch] + [dma(n) for n in sems],
        compiler_params=pltpu.CompilerParams(
            vmem_limit_bytes=LIMIT, collective_id=0, has_side_effects=True
        ),
    )(vol, cot, k1, first_bias[None], k2)
    second_out = rows_out.transpose(1, 0, 2).astype(F32) + second_bias[:, None, None]
    return (
        second_out[None, :, None],
        (scale * gw1).reshape(3, 3, 3, 32, 64).transpose(4, 3, 0, 1, 2),
        scale * gb1[0],
        (scale * gw2).reshape(3, 3, 3, 16, 64).transpose(3, 4, 0, 1, 2),
        scale * gb2[0],
    )


def solution(mesh):
    placed = (
        P("rep", None, "sx", "sy", None),
        P(),
        P(),
        P("sy", None, None, None, None),
        P("sy"),
        P("rep", "sy", "sx", None, None),
    )
    return jax.shard_map(
        per_device,
        mesh=mesh,
        in_specs=placed,
        out_specs=(
            P("rep", "sy", "sx", None, None),
            P(),
            P(),
            P("sy", None, None, None, None),
            P("sy"),
        ),
        check_vma=False,
    )
```

time: 545 us -> 68.9 us (0.13); the launches traced: 535 us -> 68.7 us
  waiting for transfers between devices: 177 us -> 0 us
  blocking collectives: 103 us -> 0 us
  local copies, waits for them, and re-layouts: 97.9 us -> 4.63 us
  matrix products: 90 us -> 0 us
  Pallas kernels: 0 us -> 58.5 us
  other arithmetic: 31.6 us -> 4.89 us
  starting transfers between devices: 21.1 us -> 0 us
  between operations: 14.8 us -> 0.67 us
    psum x2 -> x0, waiting for transfers between devices: 117 us -> none  [the longest x1 75.9 us: per_device(): summed_w2, summed_b2 = lax.psum((local_w2, local_b2), ('sx', 'rep'))]
    psum x2 -> x0, blocking collectives: 103 us -> none  [the longest x1 66.4 us: per_device(): summed_w1, summed_b1 = lax.psum((local_w1, local_b1), ('sx', 'sy', 'rep'))]
    pallas_call x0 -> x1, Pallas kernels: none -> 58.5 us  [per_device(): pl.pallas_call(whole_kernel, out_shape=tuple((jax.ShapeDtypeStruct(s, t)...]
    dot_general x54 -> x0, matrix products: 48.6 us -> none  [weight_terms(): jnp.einsum('oxyz,cxyz->oc', cotan, piece, preferred_element_type=jnp.floa...]
    conv_general_dilated x11 -> x0, local copies, waits for them, and re-layouts: 45.9 us -> none  [convolve(): lax.conv_general_dilated(padded[None], kernel, (1, 1, 1), ((0, 0), (0, 0)...]
    conv_general_dilated x3 -> x0, matrix products: 41.4 us -> none  [convolve(): lax.conv_general_dilated(padded[None], kernel, (1, 1, 1), ((0, 0), (0, 0)...]
    all_gather x1 -> x0, waiting for transfers between devices: 40.3 us -> none  [per_device(): gathered = lax.all_gather(pooled_x, 'sy', axis=2, tiled=True)]
    unnamed x51 -> x11, local copies, waits for them, and re-layouts: 25.9 us -> 4.63 us
  transfers between devices with their start and end apart: 12 -> 0, of which waited for: 9 -> 0; matrix products, arithmetic and copies ran while one was open for 33% -> 0% of each run, Pallas kernels for 0% -> 0%
where the time goes in v2:
time: 68.9 us; the launch traced here: 68.7 us
  Pallas kernels  58.5 us (85%)
  other arithmetic  4.89 us (7%)
  local copies, waits for them, and re-layouts  4.63 us (7%)
    pallas_call x1, Pallas kernels, per_device(): pl.pallas_call(whole_kernel, out_shape=tuple((jax.ShapeDtypeStruct(s, t)...  58.5 us
    unnamed x11, local copies, waits for them, and re-layouts  4.63 us
    mul x1, other arithmetic, per_device(): scale * gw2  1.64 us

profile of v2, /device:TPU:1, one launch (start us, length us, event | category | flops | bytes accessed | tf_op | source)
XLA Modules:
  0.0 68.7 jit_solution(14792764714575987143)
XLA Ops:
  0.6 0.0 copy-start
  0.6 1.9 %copy.17 = bf16[1,16,1,64,128]{4,1,3,2,0:T(8,128)(2,1)} copy(bf16[1,16,1,64,128]{4,3,2,1,0:T(8,128)(2,1)} %param.11) | data formatting | bytes 524288 | tf_op args[5]
  2.5 0.0 copy-done
  2.5 1.1 %copy.16 = bf16[1,32,2,16,256]{4,1,3,2,0:T(8,128)(2,1)} copy(bf16[1,32,2,16,256]{4,3,2,1,0:T(8,128)(2,1)S(1)} %copy-done) | data formatting | bytes 1048576 | tf_op args[0]
  3.6 58.5 %shard_map.101 = (bf16[64,16,128]{2,1,0:T(8,128)(2,1)}, f32[27,16,64]{2,1,0:T(8,128)}, f32[1,16]{1,0:T(1,128)}, f32[27,32,64]{2,1,0:T(8,128)}, f32[1,64]{1,0:T(1,128)}) custom-call(bf16[2,16,32,256]{3,2,1,0:T(8,128)(2,1)} %bitcast.31, bf16[64,16,128]{2,1,0:T(8,128)(2,1)} %bitcast.32, bf16[27,32,64]{2,1,0:T(8,128)(2,1)} %bitcast.35, f32[1,64]{1,0:T(1,128)} %bitcast.37, ...), custom_call_target="tpu_custom_call" | custom-call | tf_op jit(solution)/shard_map/pallas_call | solution.py:473
  62.1 0.0 copy-start.2
  62.1 1.2 %multiply_bitcast_fusion.1 = f32[64]{0:T(128)} fusion(f32[1,64]{1,0:T(1,128)} %get-tuple-element.12), kind=kLoop, calls=%fused_computation.6 | loop fusion | flops 64 | bytes 512 | tf_op jit(solution)/shard_map/mul | solution.py:487
  63.3 1.1 %multiply_bitcast_fusion = f32[16]{0:T(128)} fusion(f32[1,16]{1,0:T(1,128)} %get-tuple-element.14), kind=kLoop, calls=%fused_computation.5 | loop fusion | flops 16 | bytes 128 | tf_op jit(solution)/shard_map/mul | solution.py:489
  64.5 1.6 %broadcast_multiply_fusion.1 = f32[27,16,64]{2,1,0:T(8,128)} fusion(f32[27,16,64]{2,1,0:T(8,128)} %get-tuple-element.13), kind=kLoop, calls=%fused_computation.4 | loop fusion | flops 27648 | bytes 221184 | tf_op jit(solution)/shard_map/mul | solution.py:488
  66.1 0.0 copy-start.3
  66.1 0.0 copy-done.2
  66.1 0.7 copy-done.3
  66.7 0.1 add_bitcast_fusion
  66.9 0.0 copy-start.1
  66.9 1.0 %copy.13 = f32[1,16,1,64,128]{4,3,2,1,0:T(8,128)} copy(f32[1,16,1,64,128]{4,1,3,2,0:T(8,128)S(1)} %add_bitcast_fusion) | data formatting | bytes 1048576
  67.8 0.0 copy-done.1
  67.9 0.8 %broadcast_multiply_fusion = f32[27,32,64]{2,1,0:T(8,128)} fusion(f32[27,32,64]{2,1,0:T(8,128)S(1)} %copy-done.1), kind=kLoop, calls=%fused_computation.3 | loop fusion | flops 55296 | bytes 442368 | tf_op jit(solution)/shard_map/mul | solution.py:486
Async XLA Ops:
  0.6 1.9 %copy-start = (bf16[1,32,2,16,256]{4,3,2,1,0:T(8,128)(2,1)S(1)}, bf16[1,32,2,16,256]{4,3,2,1,0:T(8,128)(2,1)}, u32[]{:S(2)}) copy-start(bf16[1,32,2,16,256]{4,3,2,1,0:T(8,128)(2,1)} %param.6) | copy-start | bytes 1572868
  62.1 4.0 %copy-start.2 = (bf16[64,16,128]{2,1,0:T(8,128)(2,1)S(1)}, bf16[64,16,128]{2,1,0:T(8,128)(2,1)}, u32[]{:S(2)}) copy-start(bf16[64,16,128]{2,1,0:T(8,128)(2,1)} %get-tuple-element.10) | copy-start | bytes 786436
  66.1 0.7 copy-start.3
  66.9 1.0 %copy-start.1 = (f32[27,32,64]{2,1,0:T(8,128)S(1)}, f32[27,32,64]{2,1,0:T(8,128)}, u32[]{:S(2)}) copy-start(f32[27,32,64]{2,1,0:T(8,128)} %get-tuple-element.11) | copy-start | bytes 663556

commit v3 on v2

--- a/solution.py
+++ b/solution.py
@@ -1,3 +1,4 @@
+import functools
 import math
 
 import jax
@@ -23,13 +24,6 @@
     return pltpu.make_async_remote_copy(
         src_ref=src, dst_ref=dst, send_sem=send, recv_sem=recv, device_id=device, device_id_type=MESH
     )
-
-
-def greet(devices):
-    barrier = pltpu.get_barrier_semaphore()
-    for device in devices:
-        pl.semaphore_signal(barrier, inc=1, device_id=device, device_id_type=MESH)
-    pl.semaphore_wait(barrier, len(devices))
 
 
 def halo_copies(src, dst, send, recv):
@@ -168,28 +162,26 @@
     lax.fori_loop(0, 4, pair, 0)
 
 
-def second_grads(cot_pad, pool_pad, gw2):
+def second_grads(cot_pad, pooled, gw2):
     ones = jnp.ones((16, 256), BF16)
 
     def pair(step, carry):
         y2 = 2 * step
-        cells = jnp.concatenate([two_rows(pool_pad, y2, 64), ones], axis=0)
         own = []
         for j in range(2):
-            cot = cot_pad[1, y2 + j + 1].astype(F32)
-            own.append(
-                jnp.concatenate([shifted(cot, 1), cot, shifted(cot, -1)], axis=0).astype(BF16)
-            )
-        gw2[:, 0:592] += across(jnp.concatenate(own, axis=1), cells)
+            cells = pooled[0, y2 + j].astype(F32)
+            own.append(jnp.concatenate([shifted(cells, -1), cells, shifted(cells, 1)], axis=0).astype(BF16))
+        fields = jnp.concatenate([jnp.concatenate(own, axis=1), ones], axis=0)
+        gw2[:, 0:208] += across(two_rows(cot_pad, y2, 128), fields)
         return carry
 
     lax.fori_loop(0, 4, pair, 0)
 
 
 def whole_kernel(
-    vol, cot, k1, b1, k2, rows_out, gw2_out, gb2_out, gw1_out, gb1_out,
-    cot_src, wf_own, vol_pad, cot_pad, wf_all, w1t, w1, wbt, pooled, pool_pad, mask, second, gw1, gw2,
-    send1, recv1, part1, parts1, whole1, all1, send2, recv2, part2, parts2, whole2,
+    vol, cot, k1, b1, k2, rows_out, whole2, all1,
+    vol_src, cot_src, wf_own, vol_pad, cot_pad, wf_all, w1t, w1, wbt, pooled, pool_pad, mask, second, gw1, gw2,
+    pack1, send1, recv1, part1, parts1, whole1, pack2, send2, recv2, part2, parts2,
     ls, vs, vr, cs, cr, fs, fr, ws, wr, xs, xr, ps, pr, os_, or_,
     s1, r1, t1, q1, g1, h1, u1, v1, s2, r2, t2, q2, g2, h2,
 ):
@@ -197,49 +189,52 @@
     core = sx % 2
     left, right = (sx + 7) % 8, (sx + 1) % 8
     partner = (sx + 1 - 2 * core, sy, rep)
-    group = sx * 2 + rep
     peers = [(sx, (sy + d) % 8, rep) for d in range(1, 8)]
-    mates = []
-    for e in range(1, 16):
-        other = (group + e) % 16
-        mates.append((other // 2, sy, other % 2))
+    column = [((sx + d) % 8, sy, rep) for d in range(1, 8)]
+    group1, group2 = sy * 2 + rep, sx * 2 + rep
+    mates1, mates2 = [], []
+    for e in range(1, 16):
+        other = (group1 + e) % 16
+        mates1.append((sx, other // 2, other % 2))
+        other = (group2 + e) % 16
+        mates2.append((other // 2, sy, other % 2))
     mine = pl.ds(pl.multiple_of(16 * sy, 16), 16)
 
     def theirs(d):
         return pl.ds(pl.multiple_of(16 * ((sy + d) % 8), 16), 16)
 
+    barrier = pltpu.get_barrier_semaphore()
+    around = [((sx + (dx + 8)) % 8, (sy + (dy + 8)) % 8, rep) for dx in (-1, 1) for dy in (-1, 1)]
+    opposite = [(sx, (sy + d) % 8, 1 - rep) for d in range(1, 8)]
+    greeted = around + peers + opposite + mates2
+    for device in greeted:
+        pl.semaphore_signal(barrier, inc=1, device_id=device, device_id_type=MESH)
+    vol_src[...] = jnp.stack([jnp.swapaxes(vol[:, x], 0, 1) for x in range(2)])
     cot_src[0] = jnp.zeros((16, 128), BF16)
     cot_src[65] = jnp.zeros((16, 128), BF16)
-    cot_src[1:65] = cot[...]
+    cot_src[1:65] = jnp.swapaxes(cot[...], 0, 1)
     for k in range(9):
         for z in range(3):
             wf_own[z, :, 64 * k : 64 * k + 64] = k2[3 * k + z]
     wf_own[:, :, 576:640] = jnp.zeros((3, 16, 64), BF16)
-    greet(
-        [((sx + (dx + 8)) % 8, (sy + (dy + 8)) % 8, rep) for dx in (-1, 1) for dy in (-1, 1)]
-        + peers
-        + mates
-    )
-    halo = halo_copies(vol, vol_pad, vs, vr)
+    pl.semaphore_wait(barrier, len(greeted))
+    halo = halo_copies(vol_src, vol_pad, vs, vr)
     for copy in halo:
         copy.start()
-    exchange = []
-    for d in range(1, 8):
+    order = (4, 1, 7, 3, 5, 2, 6)
+    exchange = {}
+    for d in order:
         source = cot_src.at[pl.ds(8 * ((sy + d) % 8), 10)]
-        exchange.append(remote(source, cot_pad.at[1, :, mine, :], cs.at[d], cr.at[d], peers[d - 1]))
-    for copy in exchange:
-        copy.start()
+        exchange[d] = remote(source, cot_pad.at[1, :, mine, :], cs.at[d], cr.at[d], peers[d - 1])
+        exchange[d].start()
     planes = pl.ds(core, 2)
-    weights = []
-    for d in range(1, 8):
-        weights.append(
-            remote(wf_own.at[planes], wf_all.at[planes, mine, :], ws.at[d], wr.at[d], peers[d - 1])
-        )
-    for copy in weights:
-        copy.start()
+    weights = {}
+    for d in order:
+        weights[d] = remote(wf_own.at[planes], wf_all.at[planes, mine, :], ws.at[d], wr.at[d], peers[d - 1])
+        weights[d].start()
     own_cot = cot_src.at[pl.ds(8 * sy, 10)]
     locals_ = [
-        pltpu.make_async_copy(vol, vol_pad.at[pl.ds(1, 2), pl.ds(1, 16)], ls.at[0]),
+        pltpu.make_async_copy(vol_src, vol_pad.at[pl.ds(1, 2), pl.ds(1, 16)], ls.at[0]),
         pltpu.make_async_copy(own_cot, cot_pad.at[1, :, mine, :], ls.at[1]),
         pltpu.make_async_copy(wf_own, wf_all.at[:, mine, :], ls.at[2]),
     ]
@@ -270,33 +265,37 @@
     bias = jnp.sum(jnp.where(diagonal, b1[...], 0.0), axis=1, keepdims=True)
     gw1[...] = jnp.zeros_like(gw1)
     gw2[...] = jnp.zeros_like(gw2)
-    part1[...] = jnp.zeros_like(part1)
-    part2[...] = jnp.zeros_like(part2)
+    pack1[28:32] = jnp.zeros((4, 16, 128), F32)
+    part1[8:16] = jnp.zeros((8, 8, 128), F32)
+    part2[28:32] = jnp.zeros((4, 8, 128), F32)
     for copy in locals_ + halo:
         copy.wait()
     clear_rim(vol_pad)
-    first_rows(vol_pad, w1, bias, pooled, mask, 0, 4)
-    for d in range(1, 8):
-        exchange[d - 1].wait_recv()
+    first_rows(vol_pad, w1, bias, pooled, mask, 0, 1)
+    for d in order[:5]:
+        exchange[d].wait_recv()
         forward(d)
-    first_rows(vol_pad, w1, bias, pooled, mask, 4, 8)
-    pool_halo = halo_copies(pooled, pool_pad, ps, pr)
-    for copy in pool_halo:
-        copy.start()
-    pool_pad[1, 1:9] = pooled[0]
+    first_rows(vol_pad, w1, bias, pooled, mask, 1, 2)
+    for d in order[5:]:
+        exchange[d].wait_recv()
+        forward(d)
+    first_rows(vol_pad, w1, bias, pooled, mask, 2, 5)
     share = []
     plane = pl.ds(2 * core, 1)
-    for d in range(1, 8):
-        weights[d - 1].wait_recv()
+    for d in order:
+        weights[d].wait_recv()
         rows = theirs(8 - d)
         share.append(
             remote(wf_all.at[plane, rows, :], wf_all.at[plane, rows, :], xs.at[d], xr.at[d], partner)
         )
         share[-1].start()
-    for copy in forwards + share:
-        copy.wait()
-    for copy in exchange + weights:
-        copy.wait_send()
+    first_rows(vol_pad, w1, bias, pooled, mask, 5, 8)
+    pool_halo = halo_copies(pooled, pool_pad, ps, pr)
+    for copy in pool_halo:
+        copy.start()
+    pool_pad[1, 1:9] = pooled[0]
+    for copy in forwards:
+        copy.wait()
 
     @pl.when(sx == 0)
     def _():
@@ -306,127 +305,148 @@
     def _():
         cot_pad[2] = jnp.zeros(cot_pad.shape[1:], BF16)
 
+    second_grads(cot_pad, pooled, gw2)
+    for i in range(9):
+        pack2[i] = gw2[128 * i : 128 * (i + 1), 0:128]
+    for i in range(5):
+        last = gw2[512:640, 192:256] if i == 4 else gw2[128 * (2 * i + 1) : 128 * (2 * i + 2), 128:192]
+        pack2[9 + i] = jnp.concatenate([gw2[256 * i : 256 * i + 128, 128:192], last], axis=1)
+    send2[...] = pack2[...].astype(BF16)
+    first2 = []
+    for d in order:
+        first2.append(remote(send2.at[:, theirs(d), :], recv2.at[d], s2.at[d], r2.at[d], peers[d - 1]))
+    for copy in first2:
+        copy.start()
+    for copy in share:
+        copy.wait()
+    for d in order:
+        exchange[d].wait_send()
+        weights[d].wait_send()
     for z in range(3):
         turned = wf_all[z].T
         for k in range(9):
             wbt[64 * (2 - z) : 64 * (3 - z), 128 * (8 - k) : 128 * (9 - k)] = turned[64 * k : 64 * k + 64]
     back_rows(vol_pad, cot_pad, wbt, mask, gw1)
-    for j in range(8):
-        send1[j] = gw1[40 * j : 40 * (j + 1)].astype(BF16)
+    for i in range(18):
+        pack1[i] = gw1[16 * i : 16 * (i + 1), 0:128]
+    for i in range(9):
+        pack1[18 + i] = jnp.concatenate(
+            [gw1[16 * i : 16 * (i + 1), 128:192], gw1[144 + 16 * i : 160 + 16 * i, 128:192]], axis=1
+        )
+    pack1[27] = gw1[288:304, 0:128]
+    send1[...] = pack1[...].astype(BF16)
     first1 = []
     for d in range(1, 8):
-        first1.append(remote(send1.at[(sy + d) % 8], recv1.at[d], s1.at[d], r1.at[d], peers[d - 1]))
+        rows = pl.ds(4 * ((sx + d) % 8), 4)
+        first1.append(remote(send1.at[rows], recv1.at[d], s1.at[d], r1.at[d], column[d - 1]))
     for copy in first1:
         copy.start()
     for copy in pool_halo:
         copy.wait()
     clear_rim(pool_pad)
     second_rows(cot_pad, wf_all, pool_pad, second)
+    for copy in first1:
+        copy.wait()
+    sum1 = pack1[pl.ds(4 * sx, 4)]
+    for d in range(1, 8):
+        sum1 = sum1 + recv1[d].astype(F32)
+    for i in range(4):
+        for h in range(2):
+            part1[2 * i + h] = sum1[i, 8 * h : 8 * h + 8]
+    reduce1 = []
+    for e in range(1, 16):
+        other = (group1 + e) % 16
+        reduce1.append(remote(part1.at[other], parts1.at[e], t1.at[e], q1.at[e], mates1[e - 1]))
+    for copy in reduce1:
+        copy.start()
+    for copy in first2:
+        copy.wait()
+    sum2 = pack2[:, mine, :]
+    for d in range(1, 8):
+        sum2 = sum2 + recv2[d].astype(F32)
+    for i in range(14):
+        for h in range(2):
+            part2[2 * i + h] = sum2[i, 8 * h : 8 * h + 8]
+    reduce2 = []
+    for e in range(1, 16):
+        other = (group2 + e) % 16
+        reduce2.append(remote(part2.at[pl.ds(2 * other, 2)], parts2.at[e], t2.at[e], q2.at[e], mates2[e - 1]))
+    for copy in reduce2:
+        copy.start()
     here = pl.ds(pl.multiple_of(8 * sy, 8), 8)
     outs = []
-    for d in range(1, 8):
+    for d in order:
         outs.append(remote(second.at[:, theirs(d), :], rows_out.at[here], os_.at[d], or_.at[d], peers[d - 1]))
     for copy in outs:
         copy.start()
     kept = pltpu.make_async_copy(second.at[:, mine, :], rows_out.at[here], ls.at[3])
     kept.start()
-    second_grads(cot_pad, pool_pad, gw2)
-    send2[...] = gw2[...].reshape(3, 128, 640).astype(BF16)
-    first2 = []
-    for d in range(1, 8):
-        first2.append(remote(send2.at[:, theirs(d), :], recv2.at[d], s2.at[d], r2.at[d], peers[d - 1]))
-    for copy in first2:
-        copy.start()
-    for copy in first1:
-        copy.wait()
-    sum1 = gw1[pl.ds(pl.multiple_of(40 * sy, 8), 40), :]
-    for d in range(1, 8):
-        sum1 = sum1 + recv1[d].astype(F32)
-    for r in range(5):
-        for l in range(2):
-            part1[2 * r + l] = sum1[8 * r : 8 * r + 8, 128 * l : 128 * (l + 1)]
-    reduce1 = []
-    for e in range(1, 16):
-        other = (group + e) % 16
-        reduce1.append(remote(part1.at[other], parts1.at[e], t1.at[e], q1.at[e], mates[e - 1]))
     for copy in reduce1:
-        copy.start()
-    for copy in first2:
-        copy.wait()
-    sum2 = jnp.concatenate(
-        [gw2[pl.ds(pl.multiple_of(128 * z + 16 * sy, 16), 16), :][None] for z in range(3)], axis=0
-    )
-    for d in range(1, 8):
-        sum2 = sum2 + recv2[d].astype(F32)
-    for z in range(3):
-        for h in range(2):
-            for l in range(5):
-                part2[(z * 2 + h) * 5 + l] = sum2[z, 8 * h : 8 * h + 8, 128 * l : 128 * (l + 1)]
-    reduce2 = []
-    for e in range(1, 16):
-        other = (group + e) % 16
-        reduce2.append(remote(part2.at[pl.ds(2 * other, 2)], parts2.at[e], t2.at[e], q2.at[e], mates[e - 1]))
+        copy.wait()
+    total1 = part1[group1]
+    for e in range(1, 16):
+        total1 = total1 + parts1[e]
+    whole1[group1] = total1
+    gather1 = []
+    for e in range(1, 16):
+        gather1.append(remote(whole1.at[group1], whole1.at[group1], g1.at[e], h1.at[e], mates1[e - 1]))
+    for copy in gather1:
+        copy.start()
     for copy in reduce2:
-        copy.start()
-    for copy in reduce1:
-        copy.wait()
-    total1 = part1[group]
-    for e in range(1, 16):
-        total1 = total1 + parts1[e]
-    whole1[group] = total1
-    gather1 = []
-    for e in range(1, 16):
-        gather1.append(remote(whole1.at[group], whole1.at[group], g1.at[e], h1.at[e], mates[e - 1]))
-    for copy in gather1:
-        copy.start()
-    for copy in reduce2:
-        copy.wait()
-    own = pl.ds(2 * group, 2)
+        copy.wait()
+    own = pl.ds(2 * group2, 2)
     total2 = part2[own]
     for e in range(1, 16):
         total2 = total2 + parts2[e]
     whole2[own] = total2
     gather2 = []
     for e in range(1, 16):
-        gather2.append(remote(whole2.at[own], whole2.at[own], g2.at[e], h2.at[e], mates[e - 1]))
+        gather2.append(remote(whole2.at[own], whole2.at[own], g2.at[e], h2.at[e], mates2[e - 1]))
     for copy in gather2:
         copy.start()
     for copy in gather1:
         copy.wait()
     last1 = []
     for d in range(1, 8):
-        last1.append(remote(whole1.at[pl.ds(0, 10)], all1.at[sy], u1.at[d], v1.at[d], peers[d - 1]))
+        last1.append(remote(whole1.at[pl.ds(0, 8)], all1.at[sx], u1.at[d], v1.at[d], column[d - 1]))
     for copy in last1:
         copy.start()
-    all1[sy] = whole1[0:10]
-    for copy in gather2:
-        copy.wait()
-    for z in range(3):
-        for h in range(2):
-            for l in range(5):
-                tile = whole2[(z * 2 + h) * 5 + l]
-                gw2_out[2 * l * 3 + z, 8 * h : 8 * h + 8, :] = tile[:, 0:64]
-                if l < 4:
-                    gw2_out[(2 * l + 1) * 3 + z, 8 * h : 8 * h + 8, :] = tile[:, 64:128]
-    column = jnp.concatenate([whole2[14][:, 64:65], whole2[19][:, 64:65]], axis=0)
+    all1[sx] = whole1[0:8]
+    kept.wait()
+    for copy in outs + gather2 + last1:
+        copy.wait()
+
+
+def final_kernel(scale, rows, whole2, all1, b2, second_out, gw2_out, gb2_out, gw1_out, gb1_out):
     square = (16, 16)
     diagonal = lax.broadcasted_iota(jnp.int32, square, 0) == lax.broadcasted_iota(jnp.int32, square, 1)
+    bias = jnp.sum(jnp.where(diagonal, b2[...], 0.0), axis=1, keepdims=True)
+    second_out[...] = jnp.swapaxes(rows[...].astype(F32) + bias[None], 0, 1)
+    for h in range(2):
+        at = slice(8 * h, 8 * h + 8)
+        for i in range(9):
+            tile = whole2[2 * i + h] * scale
+            gw2_out[3 * (8 - i), at, :] = tile[:, 0:64]
+            gw2_out[3 * (8 - i) + 1, at, :] = tile[:, 64:128]
+        for i in range(5):
+            tile = whole2[2 * (9 + i) + h] * scale
+            gw2_out[3 * (8 - 2 * i) + 2, at, :] = tile[:, 0:64]
+            if i < 4:
+                gw2_out[3 * (7 - 2 * i) + 2, at, :] = tile[:, 64:128]
+    column = jnp.concatenate([whole2[26][:, 64:65], whole2[27][:, 64:65]], axis=0) * scale
     gb2_out[...] = jnp.sum(jnp.where(diagonal, column, 0.0), axis=0, keepdims=True)
-    kept.wait()
-    for copy in outs:
-        copy.wait()
-    for copy in last1:
-        copy.wait()
-    for j in range(8):
-        for r in range(5):
-            at = 40 * j + 8 * r
-            if at < 288:
-                for z in range(3):
-                    tile = all1[j, 2 * r + z // 2]
-                    gw1_out[3 * (at // 32) + z, at % 32 : at % 32 + 8, :] = tile[
-                        :, 64 * (z % 2) : 64 * (z % 2) + 64
-                    ]
-    gb1_out[...] = all1[7, 2][0:1, 64:128]
+    for i in range(27):
+        for h in range(2):
+            tile = all1[i // 4, 2 * (i % 4) + h] * scale
+            if i < 18:
+                at = 16 * i + 8 * h
+                for z in range(2):
+                    gw1_out[3 * (at // 32) + z, at % 32 : at % 32 + 8, :] = tile[:, 64 * z : 64 * z + 64]
+            else:
+                for z in range(2):
+                    at = 144 * z + 16 * (i - 18) + 8 * h
+                    gw1_out[3 * (at // 32) + 2, at % 32 : at % 32 + 8, :] = tile[:, 64 * z : 64 * z + 64]
+    gb1_out[...] = all1[6, 6][0:1, 64:128] * scale
 
 
 def dma(n):
@@ -435,14 +455,11 @@
 
 def per_device(volume, first_kernel, first_bias, second_kernel, second_bias, cotangent):
     scale = 1.0 / math.sqrt(131072)
-    vol = volume[0].transpose(1, 2, 0, 3)
-    cot = cotangent[0, :, 0].transpose(1, 0, 2)
     k1 = first_kernel.transpose(2, 3, 4, 1, 0).reshape(27, 32, 64)
     k2 = second_kernel.transpose(2, 3, 4, 0, 1).reshape(27, 16, 64)
-    outs = [
-        ((64, 16, 128), BF16), ((27, 16, 64), F32), ((1, 16), F32), ((27, 32, 64), F32), ((1, 64), F32)
-    ]
+    outs = [((64, 16, 128), BF16), ((32, 8, 128), F32), ((8, 8, 8, 128), F32)]
     scratch = [
+        ((2, 16, 32, 256), BF16),
         ((66, 16, 128), BF16),
         ((3, 16, 640), BF16),
         ((4, 18, 32, 256), BF16),
@@ -455,38 +472,45 @@
         ((3, 10, 64, 128), BF16),
         ((2, 16, 64, 256), BF16),
         ((8, 128, 128), BF16),
-        ((320, 256), F32),
-        ((384, 640), F32),
-        ((8, 40, 256), BF16),
-        ((8, 40, 256), BF16),
+        ((304, 256), F32),
+        ((1152, 256), F32),
+        ((32, 16, 128), F32),
+        ((32, 16, 128), BF16),
+        ((8, 4, 16, 128), BF16),
         ((16, 8, 128), F32),
         ((16, 8, 128), F32),
         ((16, 8, 128), F32),
-        ((8, 10, 8, 128), F32),
-        ((3, 128, 640), BF16),
-        ((8, 3, 16, 640), BF16),
+        ((14, 128, 128), F32),
+        ((14, 128, 128), BF16),
+        ((8, 14, 16, 128), BF16),
         ((32, 8, 128), F32),
         ((16, 2, 8, 128), F32),
-        ((32, 8, 128), F32),
     ]
     sems = [4, 8, 8, 8, 8, 16, 16, 8, 8, 8, 8, 8, 8, 8, 8, 8, 8, 16, 16, 16, 16, 8, 8, 8, 8, 16, 16, 16, 16]
-    rows_out, gw2, gb2, gw1, gb1 = pl.pallas_call(
+    rows, whole2, all1 = pl.pallas_call(
         whole_kernel,
         out_shape=tuple(jax.ShapeDtypeStruct(s, t) for s, t in outs),
         in_specs=[VMEM] * 5,
-        out_specs=tuple([VMEM] * 5),
+        out_specs=tuple([VMEM] * 3),
         scratch_shapes=[pltpu.VMEM(s, t) for s, t in scratch] + [dma(n) for n in sems],
         compiler_params=pltpu.CompilerParams(
             vmem_limit_bytes=LIMIT, collective_id=0, has_side_effects=True
         ),
-    )(vol, cot, k1, first_bias[None], k2)
-    second_out = rows_out.transpose(1, 0, 2).astype(F32) + second_bias[:, None, None]
+    )(volume[0], cotangent[0, :, 0], k1, first_bias[None], k2)
+    finals = [((16, 64, 128), F32), ((27, 16, 64), F32), ((1, 16), F32), ((27, 32, 64), F32), ((1, 64), F32)]
+    second_out, gw2, gb2, gw1, gb1 = pl.pallas_call(
+        functools.partial(final_kernel, scale),
+        out_shape=tuple(jax.ShapeDtypeStruct(s, t) for s, t in finals),
+        in_specs=[VMEM] * 4,
+        out_specs=tuple([VMEM] * 5),
+        compiler_params=pltpu.CompilerParams(vmem_limit_bytes=LIMIT),
+    )(rows, whole2, all1, second_bias[None])
     return (
         second_out[None, :, None],
-        (scale * gw1).reshape(3, 3, 3, 32, 64).transpose(4, 3, 0, 1, 2),
-        scale * gb1[0],
-        (scale * gw2).reshape(3, 3, 3, 16, 64).transpose(3, 4, 0, 1, 2),
-        scale * gb2[0],
+        gw1.reshape(3, 3, 3, 32, 64).transpose(4, 3, 0, 1, 2),
+        gb1[0],
+        gw2.reshape(3, 3, 3, 16, 64).transpose(3, 4, 0, 1, 2),
+        gb2[0],
     )
 
 

time: 68.9 us -> 56.3 us (0.82)
  other arithmetic: 4.89 us -> 0 us
  local copies, waits for them, and re-layouts: 4.63 us -> 0 us
  Pallas kernels: 58.5 us -> 55.5 us
    pallas_call x1, Pallas kernels: 58.5 us -> 53.2 us  [per_device(): pl.pallas_call(whole_kernel, out_shape=tuple((jax.ShapeDtypeStruct(s, t)...]
    mul x4 -> x0, other arithmetic: 4.78 us -> none  [the longest x1 1.64 us: per_device(): scale * gw2]
    unnamed x11 -> x0, local copies, waits for them, and re-layouts: 4.63 us -> none
    pallas_call x0 -> x1, Pallas kernels: none -> 2.35 us  [per_device(): pl.pallas_call(functools.partial(final_kernel, scale), out_shape=tuple((j...]
where the time goes in v3:
time: 56.3 us; the launch traced here: 56.2 us
  Pallas kernels  55.5 us (99%)
  between operations  0.64 us (1%)
    pallas_call x1, Pallas kernels, per_device(): pl.pallas_call(whole_kernel, out_shape=tuple((jax.ShapeDtypeStruct(s, t)...  53.2 us
    pallas_call x1, Pallas kernels, per_device(): pl.pallas_call(functools.partial(final_kernel, scale), out_shape=tuple((j...  2.35 us

profile of v3, /device:TPU:1, one launch (start us, length us, event | category | flops | bytes accessed | tf_op | source)
XLA Modules:
  0.0 56.2 jit_solution(15824770459697691927)
XLA Ops:
  0.6 53.2 %shard_map.101 = (bf16[64,16,128]{2,1,0:T(8,128)(2,1)}, f32[32,8,128]{2,1,0:T(8,128)}, f32[8,8,8,128]{3,2,1,0:T(8,128)}) custom-call(bf16[32,2,16,256]{3,2,1,0:T(8,128)(2,1)} %bitcast.21, bf16[16,64,128]{2,1,0:T(8,128)(2,1)} %bitcast.22, bf16[27,32,64]{2,1,0:T(8,128)(2,1)} %bitcast.23, f32[1,64]{1,0:T(1,128)} %bitcast.25, bf16[27,16,64]{2,1,0:T(8,128)(2,1)} %bitcast.24), custom_call_target="tpu_custom_call" | custom-call | tf_op jit(solution)/shard_map/pallas_call | solution.py:490
  53.8 2.3 %shard_map.102 = (f32[16,64,128]{2,1,0:T(8,128)}, f32[27,16,64]{2,1,0:T(8,128)}, f32[1,16]{1,0:T(1,128)}, f32[27,32,64]{2,1,0:T(8,128)}, f32[1,64]{1,0:T(1,128)}) custom-call(bf16[64,16,128]{2,1,0:T(8,128)(2,1)} %get-tuple-element.13.rows, f32[32,8,128]{2,1,0:T(8,128)} %get-tuple-element.14.whole2, f32[8,8,8,128]{3,2,1,0:T(8,128)} %get-tuple-element.15.all1, ...), custom_call_target="tpu_custom_call" | custom-call | tf_op jit(solution)/shard_map/pallas_call | solution.py:501

commit v4 on v3

--- a/solution.py
+++ b/solution.py
@@ -162,7 +162,7 @@
     lax.fori_loop(0, 4, pair, 0)
 
 
-def second_grads(cot_pad, pooled, gw2):
+def second_grads(cot_pad, pooled, gw2, plane):
     ones = jnp.ones((16, 256), BF16)
 
     def pair(step, carry):
@@ -172,7 +172,10 @@
             cells = pooled[0, y2 + j].astype(F32)
             own.append(jnp.concatenate([shifted(cells, -1), cells, shifted(cells, 1)], axis=0).astype(BF16))
         fields = jnp.concatenate([jnp.concatenate(own, axis=1), ones], axis=0)
-        gw2[:, 0:208] += across(two_rows(cot_pad, y2, 128), fields)
+        cots = jnp.concatenate(
+            [cot_pad[plane, pl.ds(y2 + j, 3)].reshape(384, 128) for j in range(2)], axis=1
+        )
+        gw2[384 * plane : 384 * plane + 384, 0:208] += across(cots, fields)
         return carry
 
     lax.fori_loop(0, 4, pair, 0)
@@ -181,9 +184,9 @@
 def whole_kernel(
     vol, cot, k1, b1, k2, rows_out, whole2, all1,
     vol_src, cot_src, wf_own, vol_pad, cot_pad, wf_all, w1t, w1, wbt, pooled, pool_pad, mask, second, gw1, gw2,
-    pack1, send1, recv1, part1, parts1, whole1, pack2, send2, recv2, part2, parts2,
+    pack1, send1, recv1, sums1, last1, pack2, send2, early2, late2, part2, parts2,
     ls, vs, vr, cs, cr, fs, fr, ws, wr, xs, xr, ps, pr, os_, or_,
-    s1, r1, t1, q1, g1, h1, u1, v1, s2, r2, t2, q2, g2, h2,
+    s1, r1, t1, q1, g1, h1, s2, r2, s3, r3, t2, q2, g2, h2,
 ):
     sx, sy, rep = place()
     core = sx % 2
@@ -228,10 +231,6 @@
         exchange[d] = remote(source, cot_pad.at[1, :, mine, :], cs.at[d], cr.at[d], peers[d - 1])
         exchange[d].start()
     planes = pl.ds(core, 2)
-    weights = {}
-    for d in order:
-        weights[d] = remote(wf_own.at[planes], wf_all.at[planes, mine, :], ws.at[d], wr.at[d], peers[d - 1])
-        weights[d].start()
     own_cot = cot_src.at[pl.ds(8 * sy, 10)]
     locals_ = [
         pltpu.make_async_copy(vol_src, vol_pad.at[pl.ds(1, 2), pl.ds(1, 16)], ls.at[0]),
@@ -266,8 +265,8 @@
     gw1[...] = jnp.zeros_like(gw1)
     gw2[...] = jnp.zeros_like(gw2)
     pack1[28:32] = jnp.zeros((4, 16, 128), F32)
-    part1[8:16] = jnp.zeros((8, 8, 128), F32)
-    part2[28:32] = jnp.zeros((4, 8, 128), F32)
+    pack2[5] = jnp.zeros((128, 128), F32)
+    pack2[15] = jnp.zeros((128, 128), F32)
     for copy in locals_ + halo:
         copy.wait()
     clear_rim(vol_pad)
@@ -275,11 +274,46 @@
     for d in order[:5]:
         exchange[d].wait_recv()
         forward(d)
+    weights = {}
+    for d in order:
+        weights[d] = remote(wf_own.at[planes], wf_all.at[planes, mine, :], ws.at[d], wr.at[d], peers[d - 1])
+        weights[d].start()
     first_rows(vol_pad, w1, bias, pooled, mask, 1, 2)
     for d in order[5:]:
         exchange[d].wait_recv()
         forward(d)
-    first_rows(vol_pad, w1, bias, pooled, mask, 2, 5)
+    first_rows(vol_pad, w1, bias, pooled, mask, 2, 8)
+    pool_halo = halo_copies(pooled, pool_pad, ps, pr)
+    for copy in pool_halo:
+        copy.start()
+    pool_pad[1, 1:9] = pooled[0]
+    second_grads(cot_pad, pooled, gw2, 1)
+
+    def taps(plane, row, low, high):
+        at = 384 * plane + 128 * row
+        return gw2[at : at + 128, low:high]
+
+    def both(one, other):
+        return jnp.concatenate([one, other], axis=1)
+
+    for j in range(3):
+        pack2[j] = taps(1, j, 0, 128)
+    pack2[3] = both(taps(1, 0, 128, 192), taps(1, 1, 128, 192))
+    pack2[4] = both(taps(1, 2, 128, 192), taps(1, 1, 192, 256))
+    send2[0:6] = pack2[0:6].astype(BF16)
+    first2 = []
+
+    def exchange2(start, count, landing, send, recv):
+        for e in range(1, 16):
+            other = (group1 + e) % 16
+            slots = pl.ds(start + count * (other % 2), count)
+            rows = pl.ds(pl.multiple_of(16 * (other // 2), 16), 16)
+            first2.append(
+                remote(send2.at[slots, rows, :], landing.at[e], send.at[e], recv.at[e], mates1[e - 1])
+            )
+            first2[-1].start()
+
+    exchange2(0, 3, early2, s2, r2)
     share = []
     plane = pl.ds(2 * core, 1)
     for d in order:
@@ -289,11 +323,6 @@
             remote(wf_all.at[plane, rows, :], wf_all.at[plane, rows, :], xs.at[d], xr.at[d], partner)
         )
         share[-1].start()
-    first_rows(vol_pad, w1, bias, pooled, mask, 5, 8)
-    pool_halo = halo_copies(pooled, pool_pad, ps, pr)
-    for copy in pool_halo:
-        copy.start()
-    pool_pad[1, 1:9] = pooled[0]
     for copy in forwards:
         copy.wait()
 
@@ -305,18 +334,16 @@
     def _():
         cot_pad[2] = jnp.zeros(cot_pad.shape[1:], BF16)
 
-    second_grads(cot_pad, pooled, gw2)
-    for i in range(9):
-        pack2[i] = gw2[128 * i : 128 * (i + 1), 0:128]
-    for i in range(5):
-        last = gw2[512:640, 192:256] if i == 4 else gw2[128 * (2 * i + 1) : 128 * (2 * i + 2), 128:192]
-        pack2[9 + i] = jnp.concatenate([gw2[256 * i : 256 * i + 128, 128:192], last], axis=1)
-    send2[...] = pack2[...].astype(BF16)
-    first2 = []
-    for d in order:
-        first2.append(remote(send2.at[:, theirs(d), :], recv2.at[d], s2.at[d], r2.at[d], peers[d - 1]))
-    for copy in first2:
-        copy.start()
+    second_grads(cot_pad, pooled, gw2, 0)
+    second_grads(cot_pad, pooled, gw2, 2)
+    for j in range(3):
+        pack2[6 + j] = taps(0, j, 0, 128)
+        pack2[9 + j] = taps(2, j, 0, 128)
+    pack2[12] = both(taps(0, 0, 128, 192), taps(0, 1, 128, 192))
+    pack2[13] = both(taps(0, 2, 128, 192), taps(2, 0, 128, 192))
+    pack2[14] = both(taps(2, 1, 128, 192), taps(2, 2, 128, 192))
+    send2[6:16] = pack2[6:16].astype(BF16)
+    exchange2(6, 5, late2, s3, r3)
     for copy in share:
         copy.wait()
     for d in order:
@@ -336,84 +363,76 @@
     pack1[27] = gw1[288:304, 0:128]
     send1[...] = pack1[...].astype(BF16)
     first1 = []
-    for d in range(1, 8):
-        rows = pl.ds(4 * ((sx + d) % 8), 4)
-        first1.append(remote(send1.at[rows], recv1.at[d], s1.at[d], r1.at[d], column[d - 1]))
+    for e in range(1, 16):
+        rows = pl.ds(2 * ((group1 + e) % 16), 2)
+        first1.append(remote(send1.at[rows], recv1.at[e], s1.at[e], r1.at[e], mates1[e - 1]))
     for copy in first1:
         copy.start()
     for copy in pool_halo:
         copy.wait()
     clear_rim(pool_pad)
     second_rows(cot_pad, wf_all, pool_pad, second)
-    for copy in first1:
-        copy.wait()
-    sum1 = pack1[pl.ds(4 * sx, 4)]
-    for d in range(1, 8):
-        sum1 = sum1 + recv1[d].astype(F32)
-    for i in range(4):
-        for h in range(2):
-            part1[2 * i + h] = sum1[i, 8 * h : 8 * h + 8]
-    reduce1 = []
-    for e in range(1, 16):
-        other = (group1 + e) % 16
-        reduce1.append(remote(part1.at[other], parts1.at[e], t1.at[e], q1.at[e], mates1[e - 1]))
-    for copy in reduce1:
-        copy.start()
-    for copy in first2:
-        copy.wait()
-    sum2 = pack2[:, mine, :]
-    for d in range(1, 8):
-        sum2 = sum2 + recv2[d].astype(F32)
-    for i in range(14):
-        for h in range(2):
-            part2[2 * i + h] = sum2[i, 8 * h : 8 * h + 8]
-    reduce2 = []
-    for e in range(1, 16):
-        other = (group2 + e) % 16
-        reduce2.append(remote(part2.at[pl.ds(2 * other, 2)], parts2.at[e], t2.at[e], q2.at[e], mates2[e - 1]))
-    for copy in reduce2:
-        copy.start()
     here = pl.ds(pl.multiple_of(8 * sy, 8), 8)
     outs = []
     for d in order:
         outs.append(remote(second.at[:, theirs(d), :], rows_out.at[here], os_.at[d], or_.at[d], peers[d - 1]))
-    for copy in outs:
-        copy.start()
     kept = pltpu.make_async_copy(second.at[:, mine, :], rows_out.at[here], ls.at[3])
-    kept.start()
+    for copy in first2:
+        copy.wait()
+    here2 = pack2[pl.ds(3 * rep, 3), mine, :]
+    there2 = pack2[pl.ds(6 + 5 * rep, 5), mine, :]
+    for e in range(1, 16):
+        here2 = here2 + early2[e].astype(F32)
+        there2 = there2 + late2[e].astype(F32)
+    for i in range(8):
+        for h in range(2):
+            part2[2 * i + h] = (here2[i] if i < 3 else there2[i - 3])[8 * h : 8 * h + 8]
+    reduce2 = []
+    for d in range(1, 8):
+        rows = pl.ds(2 * ((sx + d) % 8), 2)
+        reduce2.append(remote(part2.at[rows], parts2.at[d], t2.at[d], q2.at[d], column[d - 1]))
+    for copy in reduce2 + outs + [kept]:
+        copy.start()
+    for copy in first1:
+        copy.wait()
+    sum1 = pack1[pl.ds(2 * group1, 2)]
+    for e in range(1, 16):
+        sum1 = sum1 + recv1[e].astype(F32)
+    sums1[sx] = sum1
+    reduce1 = []
+    for d in range(1, 8):
+        reduce1.append(remote(sums1.at[sx], sums1.at[sx], t1.at[d], q1.at[d], column[d - 1]))
     for copy in reduce1:
-        copy.wait()
-    total1 = part1[group1]
+        copy.start()
+    for copy in reduce2:
+        copy.wait()
+    own = pl.ds(2 * sx, 2)
+    total2 = part2[own]
+    for d in range(1, 8):
+        total2 = total2 + parts2[d]
+    whole2[rep, own] = total2
+    gather2 = []
     for e in range(1, 16):
-        total1 = total1 + parts1[e]
-    whole1[group1] = total1
+        gather2.append(
+            remote(whole2.at[rep, own], whole2.at[rep, own], g2.at[e], h2.at[e], mates2[e - 1])
+        )
+    for copy in gather2:
+        copy.start()
+    for copy in reduce1:
+        copy.wait()
+    total1 = sums1[0]
+    for m in range(1, 8):
+        total1 = total1 + sums1[m]
+    last1[...] = total1.astype(BF16)
+    slots = pl.ds(2 * group1, 2)
     gather1 = []
     for e in range(1, 16):
-        gather1.append(remote(whole1.at[group1], whole1.at[group1], g1.at[e], h1.at[e], mates1[e - 1]))
+        gather1.append(remote(last1, all1.at[slots], g1.at[e], h1.at[e], mates1[e - 1]))
     for copy in gather1:
         copy.start()
-    for copy in reduce2:
-        copy.wait()
-    own = pl.ds(2 * group2, 2)
-    total2 = part2[own]
-    for e in range(1, 16):
-        total2 = total2 + parts2[e]
-    whole2[own] = total2
-    gather2 = []
-    for e in range(1, 16):
-        gather2.append(remote(whole2.at[own], whole2.at[own], g2.at[e], h2.at[e], mates2[e - 1]))
-    for copy in gather2:
-        copy.start()
-    for copy in gather1:
-        copy.wait()
-    last1 = []
-    for d in range(1, 8):
-        last1.append(remote(whole1.at[pl.ds(0, 8)], all1.at[sx], u1.at[d], v1.at[d], column[d - 1]))
-    for copy in last1:
-        copy.start()
-    all1[sx] = whole1[0:8]
+    all1[slots] = total1.astype(BF16)
     kept.wait()
-    for copy in outs + gather2 + last1:
+    for copy in outs + gather2 + gather1:
         copy.wait()
 
 
@@ -422,22 +441,33 @@
     diagonal = lax.broadcasted_iota(jnp.int32, square, 0) == lax.broadcasted_iota(jnp.int32, square, 1)
     bias = jnp.sum(jnp.where(diagonal, b2[...], 0.0), axis=1, keepdims=True)
     second_out[...] = jnp.swapaxes(rows[...].astype(F32) + bias[None], 0, 1)
-    for h in range(2):
-        at = slice(8 * h, 8 * h + 8)
-        for i in range(9):
-            tile = whole2[2 * i + h] * scale
-            gw2_out[3 * (8 - i), at, :] = tile[:, 0:64]
-            gw2_out[3 * (8 - i) + 1, at, :] = tile[:, 64:128]
-        for i in range(5):
-            tile = whole2[2 * (9 + i) + h] * scale
-            gw2_out[3 * (8 - 2 * i) + 2, at, :] = tile[:, 0:64]
-            if i < 4:
-                gw2_out[3 * (7 - 2 * i) + 2, at, :] = tile[:, 64:128]
-    column = jnp.concatenate([whole2[26][:, 64:65], whole2[27][:, 64:65]], axis=0) * scale
-    gb2_out[...] = jnp.sum(jnp.where(diagonal, column, 0.0), axis=0, keepdims=True)
+    def tap(plane, row, z):
+        return 3 * (8 - 3 * plane - row) + z
+
+    low = {0: (1, 0), 1: (1, 1), 2: (1, 2), 6: (0, 0), 7: (0, 1), 8: (0, 2), 9: (2, 0), 10: (2, 1), 11: (2, 2)}
+    high = {3: ((1, 0), (1, 1)), 4: ((1, 2), None), 12: ((0, 0), (0, 1)), 13: ((0, 2), (2, 0)), 14: ((2, 1), (2, 2))}
+    parts = []
+    for half in range(2):
+        for i in range(8):
+            slot = 3 * half + i if i < 3 else 6 + 5 * half + i - 3
+            for h in range(2):
+                at = slice(8 * h, 8 * h + 8)
+                tile = whole2[half, 2 * i + h] * scale
+                if slot in low:
+                    gw2_out[tap(*low[slot], 0), at, :] = tile[:, 0:64]
+                    gw2_out[tap(*low[slot], 1), at, :] = tile[:, 64:128]
+                elif slot in high:
+                    one, other = high[slot]
+                    gw2_out[tap(*one, 2), at, :] = tile[:, 0:64]
+                    if other:
+                        gw2_out[tap(*other, 2), at, :] = tile[:, 64:128]
+                    else:
+                        parts.append(tile[:, 64:65])
+    gb2_out[...] = jnp.sum(jnp.where(diagonal, jnp.concatenate(parts, axis=0), 0.0), axis=0, keepdims=True)
     for i in range(27):
+        block = all1[i].astype(F32) * scale
         for h in range(2):
-            tile = all1[i // 4, 2 * (i % 4) + h] * scale
+            tile = block[8 * h : 8 * h + 8]
             if i < 18:
                 at = 16 * i + 8 * h
                 for z in range(2):
@@ -446,7 +476,7 @@
                 for z in range(2):
                     at = 144 * z + 16 * (i - 18) + 8 * h
                     gw1_out[3 * (at // 32) + 2, at % 32 : at % 32 + 8, :] = tile[:, 64 * z : 64 * z + 64]
-    gb1_out[...] = all1[6, 6][0:1, 64:128] * scale
+    gb1_out[...] = all1[27].astype(F32)[0:1, 64:128] * scale
 
 
 def dma(n):
@@ -457,7 +487,7 @@
     scale = 1.0 / math.sqrt(131072)
     k1 = first_kernel.transpose(2, 3, 4, 1, 0).reshape(27, 32, 64)
     k2 = second_kernel.transpose(2, 3, 4, 0, 1).reshape(27, 16, 64)
-    outs = [((64, 16, 128), BF16), ((32, 8, 128), F32), ((8, 8, 8, 128), F32)]
+    outs = [((64, 16, 128), BF16), ((2, 16, 8, 128), F32), ((32, 16, 128), BF16)]
     scratch = [
         ((2, 16, 32, 256), BF16),
         ((66, 16, 128), BF16),
@@ -476,17 +506,17 @@
         ((1152, 256), F32),
         ((32, 16, 128), F32),
         ((32, 16, 128), BF16),
-        ((8, 4, 16, 128), BF16),
+        ((16, 2, 16, 128), BF16),
+        ((8, 2, 16, 128), F32),
+        ((2, 16, 128), BF16),
+        ((16, 128, 128), F32),
+        ((16, 128, 128), BF16),
+        ((16, 3, 16, 128), BF16),
+        ((16, 5, 16, 128), BF16),
         ((16, 8, 128), F32),
-        ((16, 8, 128), F32),
-        ((16, 8, 128), F32),
-        ((14, 128, 128), F32),
-        ((14, 128, 128), BF16),
-        ((8, 14, 16, 128), BF16),
-        ((32, 8, 128), F32),
-        ((16, 2, 8, 128), F32),
+        ((8, 2, 8, 128), F32),
     ]
-    sems = [4, 8, 8, 8, 8, 16, 16, 8, 8, 8, 8, 8, 8, 8, 8, 8, 8, 16, 16, 16, 16, 8, 8, 8, 8, 16, 16, 16, 16]
+    sems = [4] + [8] * 4 + [16] * 2 + [8] * 8 + [16] * 2 + [8] * 2 + [16] * 6 + [8] * 2 + [16] * 2
     rows, whole2, all1 = pl.pallas_call(
         whole_kernel,
         out_shape=tuple(jax.ShapeDtypeStruct(s, t) for s, t in outs),

time: 56.3 us -> 52.9 us (0.940)
  Pallas kernels: 55.5 us -> 52.1 us
    pallas_call x1, Pallas kernels: 53.2 us -> 49.8 us  [per_device(): pl.pallas_call(whole_kernel, out_shape=tuple((jax.ShapeDtypeStruct(s, t)...]
where the time goes in v4:
time: 52.9 us; the launch traced here: 52.7 us
  Pallas kernels  52.1 us (98%)
  between operations  0.64 us (1%)
    pallas_call x1, Pallas kernels, per_device(): pl.pallas_call(whole_kernel, out_shape=tuple((jax.ShapeDtypeStruct(s, t)...  49.8 us
    pallas_call x1, Pallas kernels, per_device(): pl.pallas_call(functools.partial(final_kernel, scale), out_shape=tuple((j...  2.23 us

profile of v4, /device:TPU:1, one launch (start us, length us, event | category | flops | bytes accessed | tf_op | source)
XLA Modules:
  0.0 52.7 jit_solution(13784795121522564367)
XLA Ops:
  0.6 49.8 %shard_map.101 = (bf16[64,16,128]{2,1,0:T(8,128)(2,1)}, f32[2,16,8,128]{3,2,1,0:T(8,128)}, bf16[32,16,128]{2,1,0:T(8,128)(2,1)}) custom-call(bf16[32,2,16,256]{3,2,1,0:T(8,128)(2,1)} %bitcast.21, bf16[16,64,128]{2,1,0:T(8,128)(2,1)} %bitcast.22, bf16[27,32,64]{2,1,0:T(8,128)(2,1)} %bitcast.23, f32[1,64]{1,0:T(1,128)} %bitcast.25, bf16[27,16,64]{2,1,0:T(8,128)(2,1)} %bitcast.24), custom_call_target="tpu_custom_call" | custom-call | tf_op jit(solution)/shard_map/pallas_call | solution.py:520
  50.5 2.2 %shard_map.102 = (f32[16,64,128]{2,1,0:T(8,128)}, f32[27,16,64]{2,1,0:T(8,128)}, f32[1,16]{1,0:T(1,128)}, f32[27,32,64]{2,1,0:T(8,128)}, f32[1,64]{1,0:T(1,128)}) custom-call(bf16[64,16,128]{2,1,0:T(8,128)(2,1)} %get-tuple-element.13.rows, f32[2,16,8,128]{3,2,1,0:T(8,128)} %get-tuple-element.14.whole2, bf16[32,16,128]{2,1,0:T(8,128)(2,1)} %get-tuple-element.15.all1, ...), custom_call_target="tpu_custom_call" | custom-call | tf_op jit(solution)/shard_map/pallas_call | solution.py:531

commit v5 on v4

--- a/solution.py
+++ b/solution.py
@@ -60,6 +60,11 @@
     @pl.when(sy == 7)
     def _():
         dst[:, rim_y] = jnp.zeros((dst.shape[0],) + dst.shape[2:], dst.dtype)
+
+
+def settle(region, *semaphores):
+    for semaphore in semaphores:
+        pltpu.make_async_copy(region, region, semaphore).wait()
 
 
 def shifted(block, step):
@@ -150,11 +155,10 @@
     lax.fori_loop(0, 4, pair, 0)
 
 
-def second_rows(cot_pad, wf_all, pool_pad, second):
+def second_rows(wlhs, pool_pad, second):
     def pair(step, carry):
         y2 = 2 * step
-        weights = wf_all[...].reshape(384, 640)[:, 0:576]
-        stacked = jnp.dot(weights, two_rows(pool_pad, y2, 64), preferred_element_type=F32)
+        stacked = jnp.dot(wlhs[...], two_rows(pool_pad, y2, 64), preferred_element_type=F32)
         for j in range(2):
             second[y2 + j] = combine(stacked[:, 128 * j : 128 * (j + 1)], 128).astype(BF16)
         return carry
@@ -182,10 +186,10 @@
 
 
 def whole_kernel(
-    vol, cot, k1, b1, k2, rows_out, whole2, all1,
-    vol_src, cot_src, wf_own, vol_pad, cot_pad, wf_all, w1t, w1, wbt, pooled, pool_pad, mask, second, gw1, gw2,
-    pack1, send1, recv1, sums1, last1, pack2, send2, early2, late2, part2, parts2,
-    ls, vs, vr, cs, cr, fs, fr, ws, wr, xs, xr, ps, pr, os_, or_,
+    vol_hbm, cot_hbm, k1_hbm, b1_hbm, k2_hbm, rows_out, whole2, all1,
+    vol, cot, k1, b1, k2, vol_src, cot_src, wf_own, vol_pad, cot_pad, wf_all, wlhs, w1t, w1, wbt, pooled, pool_pad, mask, second, gw1, gw2,
+    pack1, send1, recv1, half1, sums1, last1, pack2, send2, early2, late2, part2, parts2,
+    ins, ls, vs, vr, cs, cr, fs, fr, ws, wr, xs, xr, ps, pr, os_, or_,
     s1, r1, t1, q1, g1, h1, s2, r2, s3, r3, t2, q2, g2, h2,
 ):
     sx, sy, rep = place()
@@ -212,14 +216,24 @@
     greeted = around + peers + opposite + mates2
     for device in greeted:
         pl.semaphore_signal(barrier, inc=1, device_id=device, device_id_type=MESH)
+    loads = [
+        pltpu.make_async_copy(src, dst, ins.at[i])
+        for i, (src, dst) in enumerate(
+            [(vol_hbm, vol), (cot_hbm, cot), (k2_hbm, k2), (k1_hbm, k1), (b1_hbm, b1)]
+        )
+    ]
+    for copy in loads:
+        copy.start()
+    for copy in loads:
+        copy.wait()
     vol_src[...] = jnp.stack([jnp.swapaxes(vol[:, x], 0, 1) for x in range(2)])
     cot_src[0] = jnp.zeros((16, 128), BF16)
     cot_src[65] = jnp.zeros((16, 128), BF16)
     cot_src[1:65] = jnp.swapaxes(cot[...], 0, 1)
-    for k in range(9):
-        for z in range(3):
-            wf_own[z, :, 64 * k : 64 * k + 64] = k2[3 * k + z]
-    wf_own[:, :, 576:640] = jnp.zeros((3, 16, 64), BF16)
+    for p in range(27):
+        z, k = p // 9, p % 9
+        wf_own[p // 2, :, 64 * (p % 2) : 64 * (p % 2) + 64] = k2[3 * k + z]
+    wf_own[13, :, 64:128] = jnp.zeros((16, 64), BF16)
     pl.semaphore_wait(barrier, len(greeted))
     halo = halo_copies(vol_src, vol_pad, vs, vr)
     for copy in halo:
@@ -230,7 +244,7 @@
         source = cot_src.at[pl.ds(8 * ((sy + d) % 8), 10)]
         exchange[d] = remote(source, cot_pad.at[1, :, mine, :], cs.at[d], cr.at[d], peers[d - 1])
         exchange[d].start()
-    planes = pl.ds(core, 2)
+    half = pl.ds(7 * core, 7)
     own_cot = cot_src.at[pl.ds(8 * sy, 10)]
     locals_ = [
         pltpu.make_async_copy(vol_src, vol_pad.at[pl.ds(1, 2), pl.ds(1, 16)], ls.at[0]),
@@ -245,8 +259,8 @@
         rows = theirs(8 - d)
         source = cot_pad.at[1, :, rows, :] if d else own_cot
         both = [
-            remote(source, cot_pad.at[2, :, rows, :], fs.at[d], fr.at[d], (left, sy, rep)),
-            remote(source, cot_pad.at[0, :, rows, :], fs.at[8 + d], fr.at[8 + d], (right, sy, rep)),
+            remote(source, cot_pad.at[2, :, rows, :], fs.at[0], fr.at[0], (left, sy, rep)),
+            remote(source, cot_pad.at[0, :, rows, :], fs.at[1], fr.at[1], (right, sy, rep)),
         ]
         for copy in both:
             copy.start()
@@ -267,22 +281,23 @@
     pack1[28:32] = jnp.zeros((4, 16, 128), F32)
     pack2[5] = jnp.zeros((128, 128), F32)
     pack2[15] = jnp.zeros((128, 128), F32)
-    for copy in locals_ + halo:
+    for copy in locals_:
+        copy.wait()
+    for d in order[:5]:
+        exchange[d].wait_recv()
+        forward(d)
+    for copy in halo:
         copy.wait()
     clear_rim(vol_pad)
     first_rows(vol_pad, w1, bias, pooled, mask, 0, 1)
-    for d in order[:5]:
+    for d in order[5:]:
         exchange[d].wait_recv()
         forward(d)
     weights = {}
     for d in order:
-        weights[d] = remote(wf_own.at[planes], wf_all.at[planes, mine, :], ws.at[d], wr.at[d], peers[d - 1])
+        weights[d] = remote(wf_own.at[half], wf_all.at[half, mine, :], ws.at[0], wr.at[0], peers[d - 1])
         weights[d].start()
-    first_rows(vol_pad, w1, bias, pooled, mask, 1, 2)
-    for d in order[5:]:
-        exchange[d].wait_recv()
-        forward(d)
-    first_rows(vol_pad, w1, bias, pooled, mask, 2, 8)
+    first_rows(vol_pad, w1, bias, pooled, mask, 1, 8)
     pool_halo = halo_copies(pooled, pool_pad, ps, pr)
     for copy in pool_halo:
         copy.start()
@@ -309,22 +324,21 @@
             slots = pl.ds(start + count * (other % 2), count)
             rows = pl.ds(pl.multiple_of(16 * (other // 2), 16), 16)
             first2.append(
-                remote(send2.at[slots, rows, :], landing.at[e], send.at[e], recv.at[e], mates1[e - 1])
+                remote(send2.at[slots, rows, :], landing.at[e], send.at[0], recv.at[0], mates1[e - 1])
             )
             first2[-1].start()
 
     exchange2(0, 3, early2, s2, r2)
     share = []
-    plane = pl.ds(2 * core, 1)
+    settle(wf_all.at[half, pl.ds(0, 112), :], ws.at[0], wr.at[0])
     for d in order:
-        weights[d].wait_recv()
         rows = theirs(8 - d)
         share.append(
-            remote(wf_all.at[plane, rows, :], wf_all.at[plane, rows, :], xs.at[d], xr.at[d], partner)
+            remote(wf_all.at[half, rows, :], wf_all.at[half, rows, :], xs.at[0], xr.at[0], partner)
         )
         share[-1].start()
-    for copy in forwards:
-        copy.wait()
+    for side in range(2):
+        settle(cot_pad.at[2 - 2 * side], fs.at[side], fr.at[side])
 
     @pl.when(sx == 0)
     def _():
@@ -344,15 +358,14 @@
     pack2[14] = both(taps(2, 1, 128, 192), taps(2, 2, 128, 192))
     send2[6:16] = pack2[6:16].astype(BF16)
     exchange2(6, 5, late2, s3, r3)
-    for copy in share:
-        copy.wait()
+    settle(wf_all.at[half, pl.ds(0, 112), :], xs.at[0], xr.at[0])
     for d in order:
         exchange[d].wait_send()
-        weights[d].wait_send()
-    for z in range(3):
-        turned = wf_all[z].T
-        for k in range(9):
-            wbt[64 * (2 - z) : 64 * (3 - z), 128 * (8 - k) : 128 * (9 - k)] = turned[64 * k : 64 * k + 64]
+    for p in range(27):
+        z, k = p // 9, p % 9
+        turned = wf_all[p // 2].T if p % 2 == 0 else turned
+        rows = slice(64 * (p % 2), 64 * (p % 2) + 64)
+        wbt[64 * (2 - z) : 64 * (3 - z), 128 * (8 - k) : 128 * (9 - k)] = turned[rows]
     back_rows(vol_pad, cot_pad, wbt, mask, gw1)
     for i in range(18):
         pack1[i] = gw1[16 * i : 16 * (i + 1), 0:128]
@@ -362,23 +375,54 @@
         )
     pack1[27] = gw1[288:304, 0:128]
     send1[...] = pack1[...].astype(BF16)
+    high, low = split(gw1[288:304, 0:128])
+    rows = lax.broadcasted_iota(jnp.int32, (16, 128), 0)
+    send1[27] = jnp.where(rows == 0, high.astype(F32), low.astype(F32)).astype(BF16)
+    pack1[27] = jnp.where(rows == 0, gw1[288:304, 0:128], 0.0)
     first1 = []
-    for e in range(1, 16):
-        rows = pl.ds(2 * ((group1 + e) % 16), 2)
-        first1.append(remote(send1.at[rows], recv1.at[e], s1.at[e], r1.at[e], mates1[e - 1]))
+    for d in range(1, 8):
+        rows = pl.ds(4 * ((sx + d) % 8), 4)
+        first1.append(remote(send1.at[rows], recv1.at[d], s1.at[0], r1.at[0], column[d - 1]))
     for copy in first1:
         copy.start()
     for copy in pool_halo:
         copy.wait()
     clear_rim(pool_pad)
-    second_rows(cot_pad, wf_all, pool_pad, second)
+    for p in range(27):
+        z, k = p // 9, p % 9
+        piece = wf_all[p // 2, :, 64 * (p % 2) : 64 * (p % 2) + 64]
+        wlhs[128 * z : 128 * z + 128, 64 * k : 64 * k + 64] = piece
+    second_rows(wlhs, pool_pad, second)
     here = pl.ds(pl.multiple_of(8 * sy, 8), 8)
     outs = []
     for d in order:
-        outs.append(remote(second.at[:, theirs(d), :], rows_out.at[here], os_.at[d], or_.at[d], peers[d - 1]))
+        outs.append(remote(second.at[:, theirs(d), :], rows_out.at[here], os_.at[0], or_.at[0], peers[d - 1]))
     kept = pltpu.make_async_copy(second.at[:, mine, :], rows_out.at[here], ls.at[3])
-    for copy in first2:
-        copy.wait()
+    lines = lax.broadcasted_iota(jnp.int32, (16, 128), 0)
+
+    def rounded(total, buffer):
+        buffer[...] = total.astype(BF16)
+
+        @pl.when(sx == 6)
+        def _():
+            fold_high, fold_low = split(jnp.sum(total[3][0:2], axis=0, keepdims=True))
+            buffer[3] = jnp.where(lines == 0, fold_high.astype(F32), fold_low.astype(F32)).astype(BF16)
+
+    settle(recv1.at[pl.ds(1, 7)], s1.at[0], r1.at[0])
+    sum1 = pack1[pl.ds(4 * sx, 4)]
+    for d in range(1, 8):
+        sum1 = sum1 + recv1[d].astype(F32)
+    rounded(sum1, half1)
+    reduce1 = []
+    for e in range(1, 16):
+        reduce1.append(remote(half1, sums1.at[group1], t1.at[0], q1.at[0], mates1[e - 1]))
+    for copy in reduce1:
+        copy.start()
+    sums1[group1] = half1[...]
+    for copy in outs + [kept]:
+        copy.start()
+    settle(early2.at[pl.ds(1, 15)], s2.at[0], r2.at[0])
+    settle(late2.at[pl.ds(1, 15)], s3.at[0], r3.at[0])
     here2 = pack2[pl.ds(3 * rep, 3), mine, :]
     there2 = pack2[pl.ds(6 + 5 * rep, 5), mine, :]
     for e in range(1, 16):
@@ -390,22 +434,10 @@
     reduce2 = []
     for d in range(1, 8):
         rows = pl.ds(2 * ((sx + d) % 8), 2)
-        reduce2.append(remote(part2.at[rows], parts2.at[d], t2.at[d], q2.at[d], column[d - 1]))
-    for copy in reduce2 + outs + [kept]:
-        copy.start()
-    for copy in first1:
-        copy.wait()
-    sum1 = pack1[pl.ds(2 * group1, 2)]
-    for e in range(1, 16):
-        sum1 = sum1 + recv1[e].astype(F32)
-    sums1[sx] = sum1
-    reduce1 = []
-    for d in range(1, 8):
-        reduce1.append(remote(sums1.at[sx], sums1.at[sx], t1.at[d], q1.at[d], column[d - 1]))
-    for copy in reduce1:
-        copy.start()
+        reduce2.append(remote(part2.at[rows], parts2.at[d], t2.at[0], q2.at[0], column[d - 1]))
     for copy in reduce2:
-        copy.wait()
+        copy.start()
+    settle(parts2.at[pl.ds(1, 7)], t2.at[0], q2.at[0])
     own = pl.ds(2 * sx, 2)
     total2 = part2[own]
     for d in range(1, 8):
@@ -414,26 +446,26 @@
     gather2 = []
     for e in range(1, 16):
         gather2.append(
-            remote(whole2.at[rep, own], whole2.at[rep, own], g2.at[e], h2.at[e], mates2[e - 1])
+            remote(whole2.at[rep, own], whole2.at[rep, own], g2.at[0], h2.at[0], mates2[e - 1])
         )
     for copy in gather2:
         copy.start()
-    for copy in reduce1:
-        copy.wait()
-    total1 = sums1[0]
-    for m in range(1, 8):
-        total1 = total1 + sums1[m]
-    last1[...] = total1.astype(BF16)
-    slots = pl.ds(2 * group1, 2)
+    settle(sums1.at[pl.ds(0, 15)], t1.at[0], q1.at[0])
+    total1 = sums1[0].astype(F32)
+    for m in range(1, 16):
+        total1 = total1 + sums1[m].astype(F32)
+    rounded(total1, last1)
+    slots = pl.ds(4 * sx, 4)
     gather1 = []
-    for e in range(1, 16):
-        gather1.append(remote(last1, all1.at[slots], g1.at[e], h1.at[e], mates1[e - 1]))
+    for d in range(1, 8):
+        gather1.append(remote(last1, all1.at[slots], g1.at[0], h1.at[0], column[d - 1]))
     for copy in gather1:
         copy.start()
-    all1[slots] = total1.astype(BF16)
+    all1[slots] = last1[...]
     kept.wait()
-    for copy in outs + gather2 + gather1:
-        copy.wait()
+    settle(rows_out.at[pl.ds(0, 56)], os_.at[0], or_.at[0])
+    settle(pack1.at[pl.ds(0, 15)], g2.at[0], h2.at[0])
+    settle(all1.at[pl.ds(0, 28)], g1.at[0], h1.at[0])
 
 
 def final_kernel(scale, rows, whole2, all1, b2, second_out, gw2_out, gb2_out, gw1_out, gb1_out):
@@ -476,7 +508,7 @@
                 for z in range(2):
                     at = 144 * z + 16 * (i - 18) + 8 * h
                     gw1_out[3 * (at // 32) + 2, at % 32 : at % 32 + 8, :] = tile[:, 64 * z : 64 * z + 64]
-    gb1_out[...] = all1[27].astype(F32)[0:1, 64:128] * scale
+    gb1_out[...] = jnp.sum(all1[27].astype(F32)[0:2, 64:128], axis=0, keepdims=True) * scale
 
 
 def dma(n):
@@ -489,12 +521,18 @@
     k2 = second_kernel.transpose(2, 3, 4, 0, 1).reshape(27, 16, 64)
     outs = [((64, 16, 128), BF16), ((2, 16, 8, 128), F32), ((32, 16, 128), BF16)]
     scratch = [
+        ((32, 2, 16, 256), BF16),
+        ((16, 64, 128), BF16),
+        ((27, 32, 64), BF16),
+        ((1, 64), F32),
+        ((27, 16, 64), BF16),
         ((2, 16, 32, 256), BF16),
         ((66, 16, 128), BF16),
-        ((3, 16, 640), BF16),
+        ((14, 16, 128), BF16),
         ((4, 18, 32, 256), BF16),
         ((3, 10, 128, 128), BF16),
-        ((3, 128, 640), BF16),
+        ((14, 128, 128), BF16),
+        ((384, 576), BF16),
         ((384, 256), BF16),
         ((256, 384), BF16),
         ((192, 1152), BF16),
@@ -506,9 +544,10 @@
         ((1152, 256), F32),
         ((32, 16, 128), F32),
         ((32, 16, 128), BF16),
-        ((16, 2, 16, 128), BF16),
-        ((8, 2, 16, 128), F32),
-        ((2, 16, 128), BF16),
+        ((8, 4, 16, 128), BF16),
+        ((4, 16, 128), BF16),
+        ((16, 4, 16, 128), BF16),
+        ((4, 16, 128), BF16),
         ((16, 128, 128), F32),
         ((16, 128, 128), BF16),
         ((16, 3, 16, 128), BF16),
@@ -516,11 +555,11 @@
         ((16, 8, 128), F32),
         ((8, 2, 8, 128), F32),
     ]
-    sems = [4] + [8] * 4 + [16] * 2 + [8] * 8 + [16] * 2 + [8] * 2 + [16] * 6 + [8] * 2 + [16] * 2
+    sems = [5, 4] + [8] * 4 + [2] * 2 + [1] * 4 + [8] * 2 + [1] * 16
     rows, whole2, all1 = pl.pallas_call(
         whole_kernel,
         out_shape=tuple(jax.ShapeDtypeStruct(s, t) for s, t in outs),
-        in_specs=[VMEM] * 5,
+        in_specs=[pl.BlockSpec(memory_space=pl.ANY)] * 5,
         out_specs=tuple([VMEM] * 3),
         scratch_shapes=[pltpu.VMEM(s, t) for s, t in scratch] + [dma(n) for n in sems],
         compiler_params=pltpu.CompilerParams(

time: 52.9 us -> 50.6 us (0.957)
  Pallas kernels: 52.1 us -> 49.9 us
    pallas_call x1, Pallas kernels: 49.8 us -> 47.6 us  [per_device(): pl.pallas_call(whole_kernel, out_shape=tuple((jax.ShapeDtypeStruct(s, t)...]
where the time goes in v5:
time: 50.6 us; the launch traced here: 50.5 us
  Pallas kernels  49.9 us (99%)
  between operations  0.64 us (1%)
    pallas_call x1, Pallas kernels, per_device(): pl.pallas_call(whole_kernel, out_shape=tuple((jax.ShapeDtypeStruct(s, t)...  47.6 us
    pallas_call x1, Pallas kernels, per_device(): pl.pallas_call(functools.partial(final_kernel, scale), out_shape=tuple((j...  2.23 us

profile of v5, /device:TPU:1, one launch (start us, length us, event | category | flops | bytes accessed | tf_op | source)
XLA Modules:
  0.0 50.5 jit_solution(2708942951960787871)
XLA Ops:
  0.6 47.6 %shard_map.101 = (bf16[64,16,128]{2,1,0:T(8,128)(2,1)}, f32[2,16,8,128]{3,2,1,0:T(8,128)}, bf16[32,16,128]{2,1,0:T(8,128)(2,1)}) custom-call(bf16[32,2,16,256]{3,2,1,0:T(8,128)(2,1)} %bitcast.21, bf16[16,64,128]{2,1,0:T(8,128)(2,1)} %bitcast.22, bf16[27,32,64]{2,1,0:T(8,128)(2,1)} %bitcast.23, f32[1,64]{1,0:T(1,128)} %bitcast.25, bf16[27,16,64]{2,1,0:T(8,128)(2,1)} %bitcast.24), custom_call_target="tpu_custom_call" | custom-call | tf_op jit(solution)/shard_map/pallas_call | solution.py:559
  48.3 2.2 %shard_map.102 = (f32[16,64,128]{2,1,0:T(8,128)}, f32[27,16,64]{2,1,0:T(8,128)}, f32[1,16]{1,0:T(1,128)}, f32[27,32,64]{2,1,0:T(8,128)}, f32[1,64]{1,0:T(1,128)}) custom-call(bf16[64,16,128]{2,1,0:T(8,128)(2,1)} %get-tuple-element.13.rows, f32[2,16,8,128]{3,2,1,0:T(8,128)} %get-tuple-element.14.whole2, bf16[32,16,128]{2,1,0:T(8,128)(2,1)} %get-tuple-element.15.all1, ...), custom_call_target="tpu_custom_call" | custom-call | tf_op jit(solution)/shard_map/pallas_call | solution.py:570

commit v6 on v5

--- a/solution.py
+++ b/solution.py
@@ -36,8 +36,8 @@
         from_y = {1: pl.ds(cells_y - 1, 1), -1: pl.ds(0, 1), 0: pl.ds(0, cells_y)}[dy]
         to_x = {1: pl.ds(0, 1), -1: pl.ds(rim_x, 1), 0: pl.ds(1, cells_x)}[dx]
         to_y = {1: pl.ds(0, 1), -1: pl.ds(rim_y, 1), 0: pl.ds(1, cells_y)}[dy]
-        device = ((sx + (dx + 8)) % 8, (sy + (dy + 8)) % 8, rep)
-        copies.append(remote(src.at[from_x, from_y], dst.at[to_x, to_y], send.at[k], recv.at[k], device))
+        device = (lax.rem(sx + (dx + 8), 8), lax.rem(sy + (dy + 8), 8), rep)
+        copies.append(remote(src.at[from_x, from_y], dst.at[to_x, to_y], send.at[0], recv.at[0], device))
     return copies
 
 
@@ -193,26 +193,26 @@
     s1, r1, t1, q1, g1, h1, s2, r2, s3, r3, t2, q2, g2, h2,
 ):
     sx, sy, rep = place()
-    core = sx % 2
-    left, right = (sx + 7) % 8, (sx + 1) % 8
+    core = lax.rem(sx, 2)
+    left, right = lax.rem(sx + 7, 8), lax.rem(sx + 1, 8)
     partner = (sx + 1 - 2 * core, sy, rep)
-    peers = [(sx, (sy + d) % 8, rep) for d in range(1, 8)]
-    column = [((sx + d) % 8, sy, rep) for d in range(1, 8)]
+    peers = [(sx, lax.rem(sy + d, 8), rep) for d in range(1, 8)]
+    column = [(lax.rem(sx + d, 8), sy, rep) for d in range(1, 8)]
     group1, group2 = sy * 2 + rep, sx * 2 + rep
     mates1, mates2 = [], []
     for e in range(1, 16):
-        other = (group1 + e) % 16
-        mates1.append((sx, other // 2, other % 2))
-        other = (group2 + e) % 16
-        mates2.append((other // 2, sy, other % 2))
+        other = lax.rem(group1 + e, 16)
+        mates1.append((sx, lax.div(other, 2), lax.rem(other, 2)))
+        other = lax.rem(group2 + e, 16)
+        mates2.append((lax.div(other, 2), sy, lax.rem(other, 2)))
     mine = pl.ds(pl.multiple_of(16 * sy, 16), 16)
 
     def theirs(d):
-        return pl.ds(pl.multiple_of(16 * ((sy + d) % 8), 16), 16)
+        return pl.ds(pl.multiple_of(16 * (lax.rem(sy + d, 8)), 16), 16)
 
     barrier = pltpu.get_barrier_semaphore()
-    around = [((sx + (dx + 8)) % 8, (sy + (dy + 8)) % 8, rep) for dx in (-1, 1) for dy in (-1, 1)]
-    opposite = [(sx, (sy + d) % 8, 1 - rep) for d in range(1, 8)]
+    around = [(lax.rem(sx + (dx + 8), 8), lax.rem(sy + (dy + 8), 8), rep) for dx in (-1, 1) for dy in (-1, 1)]
+    opposite = [(sx, lax.rem(sy + d, 8), 1 - rep) for d in range(1, 8)]
     greeted = around + peers + opposite + mates2
     for device in greeted:
         pl.semaphore_signal(barrier, inc=1, device_id=device, device_id_type=MESH)
@@ -241,7 +241,7 @@
     order = (4, 1, 7, 3, 5, 2, 6)
     exchange = {}
     for d in order:
-        source = cot_src.at[pl.ds(8 * ((sy + d) % 8), 10)]
+        source = cot_src.at[pl.ds(8 * (lax.rem(sy + d, 8)), 10)]
         exchange[d] = remote(source, cot_pad.at[1, :, mine, :], cs.at[d], cr.at[d], peers[d - 1])
         exchange[d].start()
     half = pl.ds(7 * core, 7)
@@ -286,8 +286,7 @@
     for d in order[:5]:
         exchange[d].wait_recv()
         forward(d)
-    for copy in halo:
-        copy.wait()
+    settle(mask.at[pl.ds(0, 2), pl.ds(0, 10)], vs.at[0], vr.at[0])
     clear_rim(vol_pad)
     first_rows(vol_pad, w1, bias, pooled, mask, 0, 1)
     for d in order[5:]:
@@ -320,9 +319,9 @@
 
     def exchange2(start, count, landing, send, recv):
         for e in range(1, 16):
-            other = (group1 + e) % 16
-            slots = pl.ds(start + count * (other % 2), count)
-            rows = pl.ds(pl.multiple_of(16 * (other // 2), 16), 16)
+            other = lax.rem(group1 + e, 16)
+            slots = pl.ds(start + count * lax.rem(other, 2), count)
+            rows = pl.ds(pl.multiple_of(16 * lax.div(other, 2), 16), 16)
             first2.append(
                 remote(send2.at[slots, rows, :], landing.at[e], send.at[0], recv.at[0], mates1[e - 1])
             )
@@ -381,12 +380,11 @@
     pack1[27] = jnp.where(rows == 0, gw1[288:304, 0:128], 0.0)
     first1 = []
     for d in range(1, 8):
-        rows = pl.ds(4 * ((sx + d) % 8), 4)
+        rows = pl.ds(4 * (lax.rem(sx + d, 8)), 4)
         first1.append(remote(send1.at[rows], recv1.at[d], s1.at[0], r1.at[0], column[d - 1]))
     for copy in first1:
         copy.start()
-    for copy in pool_halo:
-        copy.wait()
+    settle(mask.at[0, pl.ds(0, 11)], ps.at[0], pr.at[0])
     clear_rim(pool_pad)
     for p in range(27):
         z, k = p // 9, p % 9
@@ -433,7 +431,7 @@
             part2[2 * i + h] = (here2[i] if i < 3 else there2[i - 3])[8 * h : 8 * h + 8]
     reduce2 = []
     for d in range(1, 8):
-        rows = pl.ds(2 * ((sx + d) % 8), 2)
+        rows = pl.ds(2 * (lax.rem(sx + d, 8)), 2)
         reduce2.append(remote(part2.at[rows], parts2.at[d], t2.at[0], q2.at[0], column[d - 1]))
     for copy in reduce2:
         copy.start()
@@ -555,7 +553,7 @@
         ((16, 8, 128), F32),
         ((8, 2, 8, 128), F32),
     ]
-    sems = [5, 4] + [8] * 4 + [2] * 2 + [1] * 4 + [8] * 2 + [1] * 16
+    sems = [5, 4] + [1] * 2 + [8] * 2 + [2] * 2 + [1] * 22
     rows, whole2, all1 = pl.pallas_call(
         whole_kernel,
         out_shape=tuple(jax.ShapeDtypeStruct(s, t) for s, t in outs),

time: 50.6 us -> 50.2 us (level)
  no operation moved by 1% of the time
where the time goes in v6:
time: 50.2 us; the launch traced here: 50.1 us
  Pallas kernels  49.4 us (98%)
  between operations  0.64 us (1%)
    pallas_call x1, Pallas kernels, per_device(): pl.pallas_call(whole_kernel, out_shape=tuple((jax.ShapeDtypeStruct(s, t)...  47.2 us
    pallas_call x1, Pallas kernels, per_device(): pl.pallas_call(functools.partial(final_kernel, scale), out_shape=tuple((j...  2.23 us

profile of v6, /device:TPU:1, one launch (start us, length us, event | category | flops | bytes accessed | tf_op | source)
XLA Modules:
  0.0 50.1 jit_solution(3905783678274864789)
XLA Ops:
  0.6 47.2 %shard_map.101 = (bf16[64,16,128]{2,1,0:T(8,128)(2,1)}, f32[2,16,8,128]{3,2,1,0:T(8,128)}, bf16[32,16,128]{2,1,0:T(8,128)(2,1)}) custom-call(bf16[32,2,16,256]{3,2,1,0:T(8,128)(2,1)} %bitcast.21, bf16[16,64,128]{2,1,0:T(8,128)(2,1)} %bitcast.22, bf16[27,32,64]{2,1,0:T(8,128)(2,1)} %bitcast.23, f32[1,64]{1,0:T(1,128)} %bitcast.25, bf16[27,16,64]{2,1,0:T(8,128)(2,1)} %bitcast.24), custom_call_target="tpu_custom_call" | custom-call | tf_op jit(solution)/shard_map/pallas_call | solution.py:557
  47.8 2.2 %shard_map.102 = (f32[16,64,128]{2,1,0:T(8,128)}, f32[27,16,64]{2,1,0:T(8,128)}, f32[1,16]{1,0:T(1,128)}, f32[27,32,64]{2,1,0:T(8,128)}, f32[1,64]{1,0:T(1,128)}) custom-call(bf16[64,16,128]{2,1,0:T(8,128)(2,1)} %get-tuple-element.13.rows, f32[2,16,8,128]{3,2,1,0:T(8,128)} %get-tuple-element.14.whole2, bf16[32,16,128]{2,1,0:T(8,128)(2,1)} %get-tuple-element.15.all1, ...), custom_call_target="tpu_custom_call" | custom-call | tf_op jit(solution)/shard_map/pallas_call | solution.py:568

commit v7 on v6

--- a/solution.py
+++ b/solution.py
@@ -283,13 +283,13 @@
     pack2[15] = jnp.zeros((128, 128), F32)
     for copy in locals_:
         copy.wait()
-    for d in order[:5]:
+    for d in order[:3]:
         exchange[d].wait_recv()
         forward(d)
     settle(mask.at[pl.ds(0, 2), pl.ds(0, 10)], vs.at[0], vr.at[0])
     clear_rim(vol_pad)
     first_rows(vol_pad, w1, bias, pooled, mask, 0, 1)
-    for d in order[5:]:
+    for d in order[3:]:
         exchange[d].wait_recv()
         forward(d)
     weights = {}

time: 50.2 us -> 49.9 us (level)
  no operation moved by 1% of the time
where the time goes in v7:
time: 49.9 us; the launch traced here: 49.7 us
  Pallas kernels  49.1 us (98%)
  between operations  0.64 us (1%)
    pallas_call x1, Pallas kernels, per_device(): pl.pallas_call(whole_kernel, out_shape=tuple((jax.ShapeDtypeStruct(s, t)...  46.8 us
    pallas_call x1, Pallas kernels, per_device(): pl.pallas_call(functools.partial(final_kernel, scale), out_shape=tuple((j...  2.23 us

profile of v7, /device:TPU:1, one launch (start us, length us, event | category | flops | bytes accessed | tf_op | source)
XLA Modules:
  0.0 49.7 jit_solution(10253953742727865728)
XLA Ops:
  0.6 46.8 %shard_map.101 = (bf16[64,16,128]{2,1,0:T(8,128)(2,1)}, f32[2,16,8,128]{3,2,1,0:T(8,128)}, bf16[32,16,128]{2,1,0:T(8,128)(2,1)}) custom-call(bf16[32,2,16,256]{3,2,1,0:T(8,128)(2,1)} %bitcast.21, bf16[16,64,128]{2,1,0:T(8,128)(2,1)} %bitcast.22, bf16[27,32,64]{2,1,0:T(8,128)(2,1)} %bitcast.23, f32[1,64]{1,0:T(1,128)} %bitcast.25, bf16[27,16,64]{2,1,0:T(8,128)(2,1)} %bitcast.24), custom_call_target="tpu_custom_call" | custom-call | tf_op jit(solution)/shard_map/pallas_call | solution.py:557
  47.5 2.2 %shard_map.102 = (f32[16,64,128]{2,1,0:T(8,128)}, f32[27,16,64]{2,1,0:T(8,128)}, f32[1,16]{1,0:T(1,128)}, f32[27,32,64]{2,1,0:T(8,128)}, f32[1,64]{1,0:T(1,128)}) custom-call(bf16[64,16,128]{2,1,0:T(8,128)(2,1)} %get-tuple-element.13.rows, f32[2,16,8,128]{3,2,1,0:T(8,128)} %get-tuple-element.14.whole2, bf16[32,16,128]{2,1,0:T(8,128)(2,1)} %get-tuple-element.15.all1, ...), custom_call_target="tpu_custom_call" | custom-call | tf_op jit(solution)/shard_map/pallas_call | solution.py:568
